TPU v7x, 32 devices: a whole 2x2x4 slice. The times are simulated.
32 devices in a mesh: seq: 4 (over z), head: 4 (over y, x), rep: 2 (over core).
Axes of the slice: x: 2, y: 2, z: 4, core: 2. Of those that a mesh axis runs over, the one named last changes fastest.
Arguments:
- moe_in: bfloat16 [1024, 2048], P(('rep', 'seq'), 'head'), parts along dimension 0, may hold values from -6 to 6
- grad_out: bfloat16 [1024, 2048], P(('rep', 'seq'), 'head'), parts along dimension 0, may hold values from -6 to 6
- routes: int32 [1024, 8], P(('rep', 'seq')), parts along dimension 0, may hold values from 0 to 63, all different within a row; in each aligned block of 128 rows (0 to 127, 128 to 255, ...) at most 18 rows name the same one
- route_weight: bfloat16 [1024, 8], P(('rep', 'seq')), parts along dimension 0, may hold values from 0.049804688 to 0.5
- w_gate: bfloat16 [64, 2048, 512], P('seq', None, 'head'), may hold values from -0.125 to 0.125
- w_up: bfloat16 [64, 2048, 512], P('seq', None, 'head'), may hold values from -0.125 to 0.125
- w_down: bfloat16 [64, 512, 2048], P('seq', 'head'), may hold values from -0.25 to 0.25
- queries: bfloat16 [1024, 2048], P(('rep', 'seq'), 'head'), parts along dimension 0, may hold values from -8 to 8
- key_value: bfloat16 [1024, 4, 128], P(('rep', 'seq'), 'head'), parts along dimension 0, may hold values from -8 to 8
Outputs:
- d_moe_in: bfloat16 [1024, 2048], P(('rep', 'seq'), 'head'), parts along dimension 0
- d_route_weight: bfloat16 [1024, 8], P(('rep', 'seq')), parts along dimension 0
- grad_gate: bfloat16 [128, 2048, 512], P(('rep', 'seq'), None, 'head'), parts along dimension 0
- grad_up: bfloat16 [128, 2048, 512], P(('rep', 'seq'), None, 'head'), parts along dimension 0
- grad_down: bfloat16 [128, 512, 2048], P(('rep', 'seq'), 'head'), parts along dimension 0
- d_queries: bfloat16 [1024, 2048], P(('rep', 'seq'), 'head'), parts along dimension 0
- d_key_value: bfloat16 [1024, 4, 128], P(('rep', 'seq'), 'head'), parts along dimension 0
There are 2 independent parts, one for each index of `rep`. A program takes and returns all parts, laid end to end along the dimension named above; an argument that names none is the same for every part. Nothing has to cross between parts.
Inputs may be any that keep to these rules, and one draw needn't show every extreme that they name: `routes`: each row names 8 different experts. In each aligned block of 128 rows (the tokens of one sequence shard) no expert is named by more than 18 rows, and in every draw some block has an expert named by exactly 18 rows.
All inputs are finite; a program needn't handle non-finite values.
Results may differ from a plain program's by a relative error of at most 0.03.
Values may be sent and summed in bfloat16 or wider, within the bound.
A program may use at most 128 MiB of HBM per device.

v0:
```python
import jax
import jax.numpy as jnp
from jax import lax
from jax.sharding import PartitionSpec as P

EXPERTS = 64
WIN = 512
CAP = 18


def shifted(block, axis, distance):
    devices = range(lax.axis_size(axis))
    route = [(i - distance, i) for i in devices if i - distance in devices]
    return lax.ppermute(block, axis, route)


def slot_tables(routes, route_weight):
    token_rows, top_count = routes.shape
    flat_expert = routes.reshape(token_rows * top_count)
    expert_ids = jnp.arange(EXPERTS, dtype=jnp.int32)
    one_hot = (flat_expert[:, None] == expert_ids[None, :]).astype(jnp.int32)
    earlier = jnp.cumsum(one_hot, axis=0) - one_hot
    slot_rank = jnp.sum(earlier * one_hot, axis=1)
    target = flat_expert * CAP + slot_rank
    slot_cells = jnp.arange(EXPERTS * CAP, dtype=jnp.int32)
    chosen = (target[None, :] == slot_cells[:, None]).astype(jnp.float32)
    by_token = jnp.sum(chosen.reshape(EXPERTS * CAP, token_rows, top_count), axis=2).astype(
        jnp.bfloat16
    )
    slot_weight = jnp.dot(
        chosen,
        route_weight.reshape(token_rows * top_count).astype(jnp.float32),
        precision=lax.Precision.HIGHEST,
    )
    return (chosen, by_token, slot_weight.astype(jnp.bfloat16).reshape(EXPERTS, CAP))


def place_rows(by_token, source):
    placed = jnp.dot(by_token, source, preferred_element_type=jnp.float32)
    return placed.astype(jnp.bfloat16).reshape(EXPERTS, CAP, source.shape[1])


def fetch_window(own_rows, reach):
    earlier_shards = [shifted(own_rows, "seq", offset) for offset in range(reach, 0, -1)]
    window = jnp.concatenate(earlier_shards + [own_rows], axis=0)
    return window


def return_window(d_window, reach, shard):
    summed = d_window[reach * shard :]
    for offset in range(1, reach + 1):
        begin = (reach - offset) * shard
        summed = summed + shifted(
            d_window[begin : begin + shard].astype(jnp.bfloat16), "seq", -offset
        ).astype(jnp.float32)
    return summed


def shards(moe_in, grad_out, routes, route_weight, w_gate, w_up, w_down, queries, key_value):
    tokens = moe_in.shape[0]
    seq_count = lax.axis_size("seq")
    local_experts = w_gate.shape[0]
    chosen, by_token, slot_weight = slot_tables(routes, route_weight)
    part_in, part_grad, got_weight = (
        lax.all_to_all(
            place_rows(by_token, moe_in), "seq", split_axis=0, concat_axis=0, tiled=True
        ),
        lax.all_to_all(
            place_rows(by_token, grad_out), "seq", split_axis=0, concat_axis=0, tiled=True
        ),
        lax.all_to_all(slot_weight, "seq", split_axis=0, concat_axis=0, tiled=True),
    )
    got_in, got_grad = (
        lax.all_gather(part_in, "head", axis=2, tiled=True),
        lax.all_gather(part_grad, "head", axis=2, tiled=True),
    )
    width = got_in.shape[2]
    rows_in = got_in.reshape(seq_count, local_experts, CAP, width)
    rows_grad = got_grad.reshape(seq_count, local_experts, CAP, width)
    scale_w = got_weight.reshape(seq_count, local_experts, CAP).astype(jnp.float32)[..., None]
    gate_pre = jnp.einsum("secd,edf->secf", rows_in, w_gate, preferred_element_type=jnp.float32)
    up_pre = jnp.einsum("secd,edf->secf", rows_in, w_up, preferred_element_type=jnp.float32)
    back_proj = jnp.einsum("secd,efd->secf", rows_grad, w_down, preferred_element_type=jnp.float32)
    sigmoid_gate = jax.nn.sigmoid(gate_pre)
    silu_gate = gate_pre * sigmoid_gate
    active = silu_gate * up_pre
    route_part = jnp.sum(active * back_proj, axis=3)
    d_active = scale_w * back_proj
    d_gate = (d_active * up_pre * sigmoid_gate * (1.0 + gate_pre * (1.0 - sigmoid_gate))).astype(
        jnp.bfloat16
    )
    d_up = (d_active * silu_gate).astype(jnp.bfloat16)
    weighted = (scale_w * active).astype(jnp.bfloat16)
    rows_back = jnp.einsum("secf,edf->secd", d_gate, w_gate, preferred_element_type=jnp.float32)
    rows_back = rows_back + jnp.einsum(
        "secf,edf->secd", d_up, w_up, preferred_element_type=jnp.float32
    )
    rows_quarter = lax.psum_scatter(
        rows_back.reshape(seq_count * local_experts, CAP, width).astype(jnp.bfloat16),
        "head",
        scatter_dimension=2,
        tiled=True,
    )
    route_sum = lax.psum(route_part, "head").astype(jnp.bfloat16)
    grad_gate = jnp.einsum(
        "secd,secf->edf", rows_in, d_gate, preferred_element_type=jnp.float32
    ).astype(jnp.bfloat16)
    grad_up = jnp.einsum(
        "secd,secf->edf", rows_in, d_up, preferred_element_type=jnp.float32
    ).astype(jnp.bfloat16)
    grad_down = jnp.einsum(
        "secf,secd->efd", weighted, rows_grad, preferred_element_type=jnp.float32
    ).astype(jnp.bfloat16)
    back_rows, back_weight = (
        lax.all_to_all(rows_quarter, "seq", split_axis=0, concat_axis=0, tiled=True),
        lax.all_to_all(
            route_sum.reshape(seq_count * local_experts, CAP),
            "seq",
            split_axis=0,
            concat_axis=0,
            tiled=True,
        ),
    )
    quarter = back_rows.shape[2]
    d_moe_in = jnp.einsum(
        "st,sd->td",
        by_token,
        back_rows.reshape(EXPERTS * CAP, quarter),
        preferred_element_type=jnp.float32,
    ).astype(jnp.bfloat16)
    d_route = jnp.dot(
        back_weight.reshape(EXPERTS * CAP).astype(jnp.float32),
        chosen,
        precision=lax.Precision.HIGHEST,
    )
    d_route_weight = d_route.astype(jnp.bfloat16).reshape(routes.shape)
    head_dim = key_value.shape[2] // 2
    per_group = queries.shape[1] // head_dim
    reach = WIN // tokens
    scale = head_dim ** (-0.5)
    d_hidden = (grad_out.astype(jnp.float32) + d_moe_in.astype(jnp.float32)).astype(jnp.bfloat16)
    query_rows = queries.reshape(tokens * per_group, head_dim)
    grad_rows = d_hidden.reshape(tokens * per_group, head_dim)
    own_rows = key_value.reshape(tokens, 2 * head_dim)
    window = fetch_window(own_rows, reach)
    key_rows = window[:, :head_dim]
    value_rows = window[:, head_dim:]
    contract_last = (((1,), (1,)), ((), ()))
    contract_first = (((0,), (0,)), ((), ()))
    seq_index = lax.axis_index("seq")
    key_pos = (seq_index - reach) * tokens + jnp.arange((reach + 1) * tokens, dtype=jnp.int32)
    row_total = tokens * per_group
    block_rows = min(512, row_total)
    block_count = row_total // block_rows

    def attend_block(index, carry):
        d_window, d_query_all = carry
        begin = (index * block_rows).astype(jnp.int32)
        query_blk = lax.dynamic_slice_in_dim(query_rows, begin, block_rows, 0)
        grad_blk = lax.dynamic_slice_in_dim(grad_rows, begin, block_rows, 0)
        scores = (
            lax.dot_general(query_blk, key_rows, contract_last, preferred_element_type=jnp.float32)
            * scale
        )
        position = (
            seq_index * tokens + (begin + jnp.arange(block_rows, dtype=jnp.int32)) // per_group
        )
        visible = (
            (key_pos[None, :] >= 0)
            & (key_pos[None, :] <= position[:, None])
            & (key_pos[None, :] > position[:, None] - WIN)
        )
        scores = jnp.where(visible, scores, -1e30)
        row_max = jnp.max(scores, axis=1, keepdims=True)
        raised = jnp.exp(scores - row_max)
        probs = raised / jnp.sum(raised, axis=1, keepdims=True)
        d_probs = lax.dot_general(
            grad_blk, value_rows, contract_last, preferred_element_type=jnp.float32
        )
        row_dot = jnp.sum(probs * d_probs, axis=1, keepdims=True)
        d_scores = (probs * (d_probs - row_dot) * scale).astype(jnp.bfloat16)
        probs_low = probs.astype(jnp.bfloat16)
        d_query_blk = jnp.dot(d_scores, key_rows, preferred_element_type=jnp.float32).astype(
            jnp.bfloat16
        )
        d_keys = lax.dot_general(
            d_scores, query_blk, contract_first, preferred_element_type=jnp.float32
        )
        d_values = lax.dot_general(
            probs_low, grad_blk, contract_first, preferred_element_type=jnp.float32
        )
        d_window = d_window + jnp.concatenate([d_keys, d_values], axis=1)
        d_query_all = lax.dynamic_update_slice_in_dim(d_query_all, d_query_blk, begin, 0)
        return (d_window, d_query_all)

    window_start = jnp.zeros(((reach + 1) * tokens, 2 * head_dim), jnp.float32)
    query_start = jnp.zeros((row_total, head_dim), jnp.bfloat16)
    d_window, d_query_all = lax.fori_loop(0, block_count, attend_block, (window_start, query_start))
    d_queries = d_query_all.reshape(tokens, per_group * head_dim)
    d_own = return_window(d_window, reach, tokens)
    d_key_value = d_own.astype(jnp.bfloat16).reshape(tokens, 1, 2 * head_dim)
    return (d_moe_in, d_route_weight, grad_gate, grad_up, grad_down, d_queries, d_key_value)


def solution(mesh):
    in_specs = (
        P(("rep", "seq"), "head"),
        P(("rep", "seq"), "head"),
        P(("rep", "seq"), None),
        P(("rep", "seq"), None),
        P("seq", None, "head"),
        P("seq", None, "head"),
        P("seq", "head", None),
        P(("rep", "seq"), "head"),
        P(("rep", "seq"), "head", None),
    )
    out_specs = (
        P(("rep", "seq"), "head"),
        P(("rep", "seq"), None),
        P(("rep", "seq"), None, "head"),
        P(("rep", "seq"), None, "head"),
        P(("rep", "seq"), "head", None),
        P(("rep", "seq"), "head"),
        P(("rep", "seq"), "head", None),
    )
    return jax.shard_map(shards, mesh=mesh, in_specs=in_specs, out_specs=out_specs, check_vma=False)
```

profile of v0, /device:TPU:0, one launch (start us, length us, event | category | flops | bytes accessed | tf_op | source)
XLA Modules:
  0.0 397.5 jit_solution(16628061853176593459)
XLA Ops:
  8.3 18.0 %reduce-window.6 = s32[64,8,128]{2,1,0:T(8,128)S(1)} reduce-window(s32[64,8,128]{2,1,0:T(8,128)S(1)} %fusion.68, s32[]{:T(128)} %constant.146.clone.1), window={size=1x1x128 pad=0_0x0_0x127_0}, to_apply=%region_0.0 | reduce-window | flops 8323072 | bytes 524292 | tf_op jit(solution)/shard_map/reduce-window
  27.8 6.0 %convert_reduce_fusion = bf16[1152,128]{1,0:T(8,128)(2,1)S(1)} fusion(s32[128,8]{0,1:T(8,128)S(1)} %multiply_add_fusion.1), kind=kLoop, calls=%fused_computation.56 | loop fusion | flops 3391488 | bytes 299008 | tf_op jit(solution)/shard_map/reduce_sum | solution.py:27
  34.6 43.2 %all_to_all.30 = bf16[64,18,512]{2,1,0:T(8,128)(2,1)} all-to-all(bf16[64,18,512]{2,1,0:T(8,128)(2,1)S(1)} %reshape.144), channel_id=1, replica_groups=mesh['seq'=4,'head'=4,'rep'=2] {'seq'}, dimensions={0} | all-to-all | bytes 2359296 | tf_op jit(solution)/shard_map/all_to_all | solution.py:65
  78.8 39.4 %all_to_all.31 = bf16[64,18,512]{2,1,0:T(8,128)(2,1)} all-to-all(bf16[64,18,512]{2,1,0:T(8,128)(2,1)S(1)} %reshape.142), channel_id=1, replica_groups=mesh['seq'=4,'head'=4,'rep'=2] {'seq'}, dimensions={0} | all-to-all | bytes 2359296 | tf_op jit(solution)/shard_map/all_to_all | solution.py:68
  119.6 8.1 %all_to_all.32 = bf16[4,2,144]{2,1,0:T(2,128)(2,1)S(1)} all-to-all(bf16[4,2,144]{2,1,0:T(2,128)(2,1)S(1)} %reshape.167), channel_id=1, replica_groups=mesh['seq'=4,'head'=4,'rep'=2] {'seq'}, dimensions={0} | all-to-all | bytes 4608 | tf_op jit(solution)/shard_map/all_to_all | solution.py:71
  127.9 19.2 %all-gather.5.cloned.1.call-done = bf16[64,18,2048]{2,1,0:T(8,128)(2,1)} async-done(((bf16[64,18,512]{2,1,0:T(8,128)(2,1)}), bf16[64,18,2048]{2,1,0:T(8,128)(2,1)}) %all-gather.5.cloned.1.call-update) | async-done | bytes 4718608 | tf_op jit(solution)/shard_map/all_gather | solution.py:74
  147.1 7.7 %fusion.46 = f32[4,16,18,128]{3,2,0,1:T(8,128)S(1)} fusion(bf16[16,2048,128]{2,1,0:T(8,128)(2,1)} %param.16, bf16[4,16,18,2048]{3,2,1,0:T(8,128)(2,1)} %bitcast.115), kind=kOutput, calls=%fused_computation.66 | convolution fusion | flops 603979776 | bytes 13697024 | tf_op jit(solution)/shard_map/secd,edf->secf/dot_general | solution.py:82
  154.8 6.9 %fusion.56 = f32[4,16,18,128]{3,2,0,1:T(8,128)S(1)} fusion(bf16[16,2048,128]{2,1,0:T(8,128)(2,1)} %param.15, bf16[4,16,18,2048]{3,2,1,0:T(8,128)(2,1)S(1)} %bitcast.118), kind=kOutput, calls=%fused_computation.68 | convolution fusion | flops 603979776 | bytes 13697024 | tf_op jit(solution)/shard_map/secd,edf->secf/dot_general | solution.py:81
  161.7 57.2 %all-gather.3.cloned.1.call-done = bf16[64,18,2048]{2,1,0:T(8,128)(2,1)} async-done(((bf16[64,18,512]{2,1,0:T(8,128)(2,1)}), bf16[64,18,2048]{2,1,0:T(8,128)(2,1)}) %all-gather.3.cloned.1.call-update) | async-done | bytes 4718608 | tf_op jit(solution)/shard_map/all_gather | solution.py:75
  218.8 8.3 %multiply_reduce_fusion.1 = (f32[4,16,18]{2,0,1:T(4,128)S(1)}, bf16[4,16,18,128]{3,2,0,1:T(8,128)(2,1)S(1)}, bf16[4,16,18,128]{3,2,0,1:T(8,128)(2,1)S(1)}) fusion(f32[4,16,18,128]{3,2,0,1:T(8,128)S(1)} %fusion.46, f32[4,16,18,128]{3,2,0,1:T(8,128)S(1)} %fusion.56, f32[4,16,18]{2,0,1:T(4,128)S(1)} %copy.140, bf16[16,128,2048]{2,1,0:T(8,128)(2,1)} %param.17, ...), kind=kOutput, calls=%fused_computation.72 | convolution fusion | flops 606485376 | bytes 14885888 | tf_op jit(solution)/shard_map/secd,efd->secf/dot_general | solution.py:83
  227.2 13.3 %fusion.23 = f32[16,4,18,2048]{3,2,1,0:T(8,128)} fusion(bf16[4,16,18,128]{3,2,0,1:T(8,128)(2,1)S(1)} %get-tuple-element.334, bf16[16,2048,128]{2,1,0:T(8,128)(2,1)} %param.15), kind=kOutput, calls=%fused_computation.40 | convolution fusion | flops 603979776 | bytes 18120704 | tf_op jit(solution)/shard_map/secf,edf->secd/dot_general | solution.py:94
  240.5 15.1 %fusion.33 = bf16[4,16,18,2048]{3,2,0,1:T(8,128)(2,1)} fusion(f32[16,4,18,2048]{3,2,1,0:T(8,128)} %fusion.23, bf16[4,16,18,128]{3,2,0,1:T(8,128)(2,1)S(1)} %get-tuple-element.335, bf16[16,2048,128]{2,1,0:T(8,128)(2,1)} %param.16), kind=kOutput, calls=%fused_computation.50 | convolution fusion | flops 608698368 | bytes 22839296 | tf_op jit(solution)/shard_map/secf,edf->secd/dot_general | solution.py:95
  255.6 7.6 %copy.146 = bf16[4,16,18,2048]{3,1,0,2:T(8,128)(2,1)} copy(bf16[4,16,18,2048]{3,2,0,1:T(8,128)(2,1)} %fusion.33) | data formatting | bytes 9437184 | tf_op jit(solution)/shard_map/convert_element_type | solution.py:99
  264.5 5.2 %collective-permute-start.1 = (bf16[128,128]{1,0:T(8,128)(2,1)S(1)}, bf16[128,128]{1,0:T(8,128)(2,1)S(1)}, u32[]{:S(2)}, u32[]{:S(2)}) collective-permute-start(bf16[128,128]{1,0:T(8,128)(2,1)S(1)} %bitcast.110), channel_id=1, source_target_pairs={{0,24},{1,25},{2,26},{3,27},{4,28},{5,29},{6,30},{7,31}} | collective-permute-start | bytes 98312 | tf_op jit(solution)/shard_map/ppermute | solution.py:14
  275.9 17.0 %psum.7 = bf16[4,16,18]{2,0,1:T(4,128)(2,1)S(1)} all-reduce(f32[4,16,18]{2,0,1:T(4,128)S(1)} %get-tuple-element.333), channel_id=1, replica_groups=mesh['seq'=4,'head'=4,'rep'=2] {'head'}, use_global_device_ids=true, to_apply=%region_6.7 | all-reduce | flops 1152 | bytes 6912 | tf_op jit(solution)/shard_map/psum | solution.py:104
  293.6 3.6 all-to-all-start.4
  297.2 8.9 %bitcast_convert_fusion = bf16[16,128,2048]{2,1,0:T(8,128)(2,1)} fusion(bf16[4,16,18,2048]{3,2,1,0:T(8,128)(2,1)} %bitcast.107, f32[4,16,18]{2,0,1:T(4,128)S(1)} %copy.140, f32[4,16,18,128]{3,2,0,1:T(8,128)S(1)} %fusion.46, f32[4,16,18,128]{3,2,0,1:T(8,128)S(1)} %fusion.56), kind=kOutput, calls=%fused_computation.36 | convolution fusion | flops 609206272 | bytes 14291456 | tf_op jit(solution)/shard_map/secf,secd->efd/dot_general | solution.py:111
  306.1 15.2 %reduce-scatter.2.cloned.1.call-done = bf16[64,18,512]{2,0,1:T(8,128)(2,1)} async-done(((bf16[64,18,2048]{2,0,1:T(8,128)(2,1)}), bf16[64,18,512]{2,0,1:T(8,128)(2,1)}) %reduce-scatter.2.cloned.1.call-update) | async-done | bytes 1179664 | tf_op jit(solution)/shard_map/reduce_scatter | solution.py:98
  321.3 3.1 copy.147
  324.4 4.6 %all-to-all-start.3 = ((bf16[64,18,512]{2,1,0:T(8,128)(2,1)}), bf16[64,18,512]{2,1,0:T(8,128)(2,1)S(1)}, u32[]{:S(2)}, u32[]{:S(2)}) async-start(bf16[64,18,512]{2,1,0:T(8,128)(2,1)} %copy.147), calls=%async_computation.4 | async-start | bytes 3145728 | tf_op jit(solution)/shard_map/all_to_all | solution.py:115
  329.0 8.8 %bitcast_convert_fusion.1 = bf16[16,2048,128]{2,1,0:T(8,128)(2,1)} fusion(bf16[4,16,18,128]{3,2,0,1:T(8,128)(2,1)S(1)} %get-tuple-element.335, bf16[4,16,18,2048]{3,2,1,0:T(8,128)(2,1)} %bitcast.116), kind=kOutput, calls=%fused_computation.37 | convolution fusion | flops 608174080 | bytes 13402112 | tf_op jit(solution)/shard_map/secd,secf->edf/dot_general | solution.py:108
  337.8 8.8 %bitcast_convert_fusion.2 = bf16[16,2048,128]{2,1,0:T(8,128)(2,1)} fusion(bf16[4,16,18,128]{3,2,0,1:T(8,128)(2,1)S(1)} %copy-done.6, bf16[4,16,18,2048]{3,2,1,0:T(8,128)(2,1)} %bitcast.117), kind=kOutput, calls=%fused_computation.38 | convolution fusion | flops 608174080 | bytes 13402112 | tf_op jit(solution)/shard_map/secd,secf->edf/dot_general | solution.py:105
  346.8 19.0 %all-to-all-done.3 = bf16[64,18,512]{2,1,0:T(8,128)(2,1)S(1)} async-done(((bf16[64,18,512]{2,1,0:T(8,128)(2,1)}), bf16[64,18,512]{2,1,0:T(8,128)(2,1)S(1)}, u32[]{:S(2)}, u32[]{:S(2)}) %all-to-all-start.3) | async-done | bytes 1179680 | tf_op jit(solution)/shard_map/all_to_all | solution.py:115
  368.4 10.3 %while.18 = (s32[]{:T(128)}, f32[640,128]{0,1:T(8,128)S(1)}, bf16[1024,64]{0,1:T(8,128)(2,1)S(1)}, s32[]{:T(128)}, bf16[1024,64]{1,0:T(8,128)(2,1)}, /*index=5*/...) while((s32[]{:T(128)}, f32[640,128]{0,1:T(8,128)S(1)}, ...), condition=%wide.region_11.12_spmd.clone, body=%wide.region_7.11_spmd.clone.sunk | while | flops 217212288 | bytes 13930997 | solution.py:198
  (120 shorter events, 39.0 us)
Async XLA Ops:
  7.2 26.6 %copy-start = (bf16[128,512]{1,0:T(8,128)(2,1)S(1)}, bf16[128,512]{1,0:T(8,128)(2,1)}, u32[]{:S(2)}) copy-start(bf16[128,512]{1,0:T(8,128)(2,1)} %param.11) | copy-start | bytes 393220
  7.2 139.9 %all-gather.5.cloned.1.call-start = ((), (), s32[]{:S(2)}) async-start(), calls=%async_computation.7 | async-start | bytes 7864320 | tf_op jit(solution)/shard_map/all_gather | solution.py:74
  27.0 51.0 %copy-start.4 = (bf16[128,512]{1,0:T(8,128)(2,1)S(1)}, bf16[128,512]{1,0:T(8,128)(2,1)}, u32[]{:S(2)}) copy-start(bf16[128,512]{1,0:T(8,128)(2,1)} %param.12) | copy-start | bytes 393220
  33.8 44.6 %copy-start.2 = (bf16[1152,128]{1,0:T(8,128)(2,1)}, bf16[1152,128]{1,0:T(8,128)(2,1)S(1)}, u32[]{:S(2)}) copy-start(bf16[1152,128]{1,0:T(8,128)(2,1)S(1)} %convert_reduce_fusion) | copy-start | bytes 884740
  77.9 40.4 %copy-start.9 = (bf16[128,8]{0,1:T(8,128)(2,1)S(1)}, bf16[128,8]{0,1:T(8,128)(2,1)}, u32[]{:S(2)}) copy-start(bf16[128,8]{0,1:T(8,128)(2,1)} %param.14) | copy-start | bytes 6148
  77.9 140.9 %all-gather.3.cloned.1.call-start = ((), (), s32[]{:S(2)}) async-start(), calls=%async_computation.6 | async-start | bytes 7864320 | tf_op jit(solution)/shard_map/all_gather | solution.py:75
  118.2 203.1 %reduce-scatter.2.cloned.1.call-start = ((), (), s32[]{:S(2)}) async-start(), calls=%async_computation.8 | async-start | bytes 5898240 | tf_op jit(solution)/shard_map/reduce_scatter | solution.py:98
  147.1 7.7 %copy-start.10 = (bf16[64,18,2048]{2,1,0:T(8,128)(2,1)S(1)}, bf16[64,18,2048]{2,1,0:T(8,128)(2,1)}, u32[]{:S(2)}) copy-start(bf16[64,18,2048]{2,1,0:T(8,128)(2,1)} %all-gather.5.cloned.1.call-done) | copy-start | bytes 14155780
  227.2 13.3 %copy-start.5 = (bf16[4,16,18,128]{3,2,0,1:T(8,128)(2,1)}, bf16[4,16,18,128]{3,2,0,1:T(8,128)(2,1)S(1)}, u32[]{:S(2)}) copy-start(bf16[4,16,18,128]{3,2,0,1:T(8,128)(2,1)S(1)} %get-tuple-element.334) | copy-start | bytes 884740
  263.1 10.4 %copy-start.7 = (bf16[128,512]{1,0:T(8,128)(2,1)S(1)}, bf16[128,512]{1,0:T(8,128)(2,1)}, u32[]{:S(2)}) copy-start(bf16[128,512]{1,0:T(8,128)(2,1)} %param.18) | copy-start | bytes 393220
  263.9 10.6 %collective-permute-start = (bf16[128,128]{1,0:T(8,128)(2,1)S(1)}, bf16[128,128]{1,0:T(8,128)(2,1)S(1)}, u32[]{:S(2)}, u32[]{:S(2)}) collective-permute-start(bf16[128,128]{1,0:T(8,128)(2,1)S(1)} %bitcast.109), channel_id=1, source_target_pairs={} | collective-permute-start | bytes 98312 | tf_op jit(solution)/shard_map/ppermute | solution.py:14
  264.5 10.0 %collective-permute-start.1 = (bf16[128,128]{1,0:T(8,128)(2,1)S(1)}, bf16[128,128]{1,0:T(8,128)(2,1)S(1)}, u32[]{:S(2)}, u32[]{:S(2)}) collective-permute-start(bf16[128,128]{1,0:T(8,128)(2,1)S(1)} %bitcast.110), channel_id=1, source_target_pairs={{0,24},{1,25},{2,26},{3,27},{4,28},{5,29},{6,30},{7,31}} | collective-permute-start | bytes 98312 | tf_op jit(solution)/shard_map/ppermute | solution.py:14
  269.8 4.7 %collective-permute-start.2 = (bf16[128,128]{1,0:T(8,128)(2,1)S(1)}, bf16[128,128]{1,0:T(8,128)(2,1)S(1)}, u32[]{:S(2)}, u32[]{:S(2)}) collective-permute-start(bf16[128,128]{1,0:T(8,128)(2,1)S(1)} %bitcast.111), channel_id=1, source_target_pairs={{0,16},{8,24},{1,17},{9,25},{2,18},{10,26},{3,19},{11,27},{4,20},{... | collective-permute-start | bytes 98312 | tf_op jit(solution)/shard_map/ppermute | solution.py:14
  271.1 4.1 %collective-permute-start.3 = (bf16[128,128]{1,0:T(8,128)(2,1)S(1)}, bf16[128,128]{1,0:T(8,128)(2,1)S(1)}, u32[]{:S(2)}, u32[]{:S(2)}) collective-permute-start(bf16[128,128]{1,0:T(8,128)(2,1)S(1)} %bitcast.112), channel_id=1, source_target_pairs={{0,8},{8,16},{16,24},{1,9},{9,17},{17,25},{2,10},{10,18},{18,26},{... | collective-permute-start | bytes 98312 | tf_op jit(solution)/shard_map/ppermute | solution.py:14
  293.6 30.8 %all-to-all-start.4 = ((bf16[4,2,144]{2,1,0:T(2,128)(2,1)}), bf16[4,2,144]{2,1,0:T(2,128)(2,1)S(1)}, u32[]{:S(2)}, u32[]{:S(2)}) async-start(bf16[4,2,144]{2,1,0:T(2,128)(2,1)} %reshape.169), calls=%async_computation.5 | async-start | bytes 8192 | tf_op jit(solution)/shard_map/all_to_all | solution.py:116
  324.4 41.4 %all-to-all-start.3 = ((bf16[64,18,512]{2,1,0:T(8,128)(2,1)}), bf16[64,18,512]{2,1,0:T(8,128)(2,1)S(1)}, u32[]{:S(2)}, u32[]{:S(2)}) async-start(bf16[64,18,512]{2,1,0:T(8,128)(2,1)} %copy.147), calls=%async_computation.4 | async-start | bytes 3145728 | tf_op jit(solution)/shard_map/all_to_all | solution.py:115
  329.0 8.8 %copy-start.6 = (bf16[4,16,18,128]{3,2,0,1:T(8,128)(2,1)S(1)}, bf16[4,16,18,128]{3,2,0,1:T(8,128)(2,1)}, u32[]{:S(2)}) copy-start(bf16[4,16,18,128]{3,2,0,1:T(8,128)(2,1)} %copy-done.5) | copy-start | bytes 884740
  370.4 2.0 copy-start.3
  375.5 2.0 copy-start.3
  378.7 12.3 %copy-start.1 = (bf16[128,512]{1,0:T(8,128)(2,1)S(1)}, bf16[128,512]{1,0:T(8,128)(2,1)}, u32[]{:S(2)}) copy-start(bf16[128,512]{1,0:T(8,128)(2,1)} %param.11) | copy-start | bytes 393220
  378.9 7.3 %collective-permute-start.4 = (bf16[128,128]{1,0:T(8,128)(2,1)S(1)}, bf16[128,128]{1,0:T(8,128)(2,1)S(1)}, u32[]{:S(2)}, u32[]{:S(2)}) collective-permute-start(bf16[128,128]{1,0:T(8,128)(2,1)S(1)} %get-tuple-element.336), channel_id=1, source_target_pairs={{8,0},{16,8},{24,16},{9,1},{17,9},{25,17},{10,2},{18,10},{26,18},{... | collective-permute-start | bytes 98312 | tf_op jit(solution)/shard_map/ppermute | solution.py:14
  380.2 7.0 %collective-permute-start.5 = (bf16[128,128]{1,0:T(8,128)(2,1)S(1)}, bf16[128,128]{1,0:T(8,128)(2,1)S(1)}, u32[]{:S(2)}, u32[]{:S(2)}) collective-permute-start(bf16[128,128]{1,0:T(8,128)(2,1)S(1)} %get-tuple-element.339), channel_id=1, source_target_pairs={{16,0},{24,8},{17,1},{25,9},{18,2},{26,10},{19,3},{27,11},{20,4},{... | collective-permute-start | bytes 98312 | tf_op jit(solution)/shard_map/ppermute | solution.py:14
  381.5 8.8 %collective-permute-start.6 = (bf16[128,128]{1,0:T(8,128)(2,1)S(1)}, bf16[128,128]{1,0:T(8,128)(2,1)S(1)}, u32[]{:S(2)}, u32[]{:S(2)}) collective-permute-start(bf16[128,128]{1,0:T(8,128)(2,1)S(1)} %get-tuple-element.338), channel_id=1, source_target_pairs={{24,0},{25,1},{26,2},{27,3},{28,4},{29,5},{30,6},{31,7}} | collective-permute-start | bytes 98312 | tf_op jit(solution)/shard_map/ppermute | solution.py:14
  382.8 7.5 %collective-permute-start.7 = (bf16[128,128]{1,0:T(8,128)(2,1)S(1)}, bf16[128,128]{1,0:T(8,128)(2,1)S(1)}, u32[]{:S(2)}, u32[]{:S(2)}) collective-permute-start(bf16[128,128]{1,0:T(8,128)(2,1)S(1)} %get-tuple-element.337), channel_id=1, source_target_pairs={} | collective-permute-start | bytes 98312 | tf_op jit(solution)/shard_map/ppermute | solution.py:14
  (1 other events, 0.8 us)
Sparse Core Ops, SparseCore 0:
  78.0 69.0 all-gather.4
  148.9 69.8 all-gather.2
  263.3 58.0 reduce-scatter.1
where the time goes:
time: 398 us; the launch traced here: 397 us
  waiting for transfers between devices  115 us (29%)
  blocking collectives  108 us (27%)
  matrix products  90.7 us (23%)
  other arithmetic  27.5 us (7%)
  starting transfers between devices  22.5 us (6%)
  local copies, waits for them, and re-layouts  19.5 us (5%)
  between operations  14.2 us (4%)
    all_gather x1, waiting for transfers between devices, shards(): lax.all_gather(part_grad, 'head', axis=2, tiled=True)  57.2 us
    all_to_all x1, blocking collectives, shards(): lax.all_to_all(place_rows(by_token, moe_in), 'seq', split_axis=0, concat_...  43.2 us
    all_to_all x1, blocking collectives, shards(): lax.all_to_all(place_rows(by_token, grad_out), 'seq', split_axis=0, conca...  39.4 us
    all_gather x1, waiting for transfers between devices, shards(): lax.all_gather(part_in, 'head', axis=2, tiled=True)  19.2 us
    all_to_all x1, waiting for transfers between devices, shards(): lax.all_to_all(rows_quarter, 'seq', split_axis=0, concat_axis=0, tiled=True)  19 us
    another operation x4, other arithmetic  18.2 us
    psum x1, blocking collectives, shards(): route_sum = lax.psum(route_part, 'head').astype(jnp.bfloat16)  17 us
    reduce_scatter x1, waiting for transfers between devices, shards(): lax.psum_scatter(rows_back.reshape(seq_count * local_experts, CAP, width)...  15.2 us
  transfers between devices with their start and end apart: 13, of which 7 were waited for; matrix products, arithmetic and copies ran while one was open for 13% of the time, Pallas kernels for 0%

commit v1 on v0

--- a/solution.py
+++ b/solution.py
@@ -1,6 +1,8 @@
 import jax
 import jax.numpy as jnp
 from jax import lax
+from jax.experimental import pallas as pl
+from jax.experimental.pallas import tpu as pltpu
 from jax.sharding import PartitionSpec as P
 
 EXPERTS = 64
@@ -56,8 +58,7 @@
     return summed
 
 
-def shards(moe_in, grad_out, routes, route_weight, w_gate, w_up, w_down, queries, key_value):
-    tokens = moe_in.shape[0]
+def dispatched_experts(moe_in, grad_out, routes, route_weight, w_gate, w_up, w_down):
     seq_count = lax.axis_size("seq")
     local_experts = w_gate.shape[0]
     chosen, by_token, slot_weight = slot_tables(routes, route_weight)
@@ -134,9 +135,14 @@
         precision=lax.Precision.HIGHEST,
     )
     d_route_weight = d_route.astype(jnp.bfloat16).reshape(routes.shape)
+    return (d_moe_in, d_route_weight, grad_gate, grad_up, grad_down)
+
+
+def attention(grad_out, d_moe_in, queries, key_value):
+    tokens = grad_out.shape[0]
     head_dim = key_value.shape[2] // 2
     per_group = queries.shape[1] // head_dim
-    reach = WIN // tokens
+    reach = min(WIN // tokens, lax.axis_size("seq") - 1)
     scale = head_dim ** (-0.5)
     d_hidden = (grad_out.astype(jnp.float32) + d_moe_in.astype(jnp.float32)).astype(jnp.bfloat16)
     query_rows = queries.reshape(tokens * per_group, head_dim)
@@ -199,6 +205,167 @@
     d_queries = d_query_all.reshape(tokens, per_group * head_dim)
     d_own = return_window(d_window, reach, tokens)
     d_key_value = d_own.astype(jnp.bfloat16).reshape(tokens, 1, 2 * head_dim)
+    return (d_queries, d_key_value)
+
+
+def dot(a, b, contract):
+    return lax.dot_general(a, b, (contract, ((), ())), preferred_element_type=jnp.float32)
+
+
+def expert_kernel(
+    routes_ref,
+    weight_ref,
+    x_ref,
+    dy_ref,
+    wg_ref,
+    wu_ref,
+    wd_ref,
+    gg_ref,
+    gu_ref,
+    gd_ref,
+    dmoe_ref,
+    droute_ref,
+    rank_ref,
+    dense_ref,
+    pick_ref,
+    back_ref,
+):
+    expert = pl.program_id(0)
+    experts = pl.num_programs(0)
+    heads, total, quarter = x_ref.shape
+    hidden = wg_ref.shape[2]
+    rows = pick_ref.shape[0] // rank_ref.shape[0]
+    local = rank_ref.shape[0]
+
+    @pl.when(expert == 0)
+    def _():
+        for index in range(local):
+            hit = routes_ref[...] == index
+            named = jnp.sum(hit.astype(jnp.float32), axis=0, keepdims=True)
+            rank_ref[pl.ds(index, 1), :] = named
+            dense_ref[pl.ds(index, 1), :] = jnp.sum(
+                jnp.where(hit, weight_ref[...], 0.0), axis=0, keepdims=True
+            )
+        named = rank_ref[...]
+        before = lax.broadcasted_iota(jnp.int32, (total, total), 0)
+        after = lax.broadcasted_iota(jnp.int32, (total, total), 1)
+        order = (before < after).astype(jnp.float32).astype(jnp.bfloat16)
+        earlier = dot(named.astype(jnp.bfloat16), order, ((1,), (0,)))
+        rank_ref[...] = jnp.where(named > 0.5, earlier, -1.0)
+        droute_ref[...] = jnp.zeros_like(droute_ref)
+
+    slots = lax.broadcasted_iota(jnp.int32, (rows, total), 0).astype(jnp.float32)
+    chosen = rank_ref[pl.ds(expert, 1), :] == slots
+    pick = chosen.astype(jnp.float32).astype(jnp.bfloat16)
+    start = pl.multiple_of(expert * rows, rows)
+    pick_ref[pl.ds(start, rows), :] = pick
+    scale_w = jnp.sum(
+        jnp.where(chosen, dense_ref[pl.ds(expert, 1), :], 0.0), axis=1, keepdims=True
+    )
+    x = jnp.concatenate(
+        [dot(pick, x_ref[h], ((1,), (0,))).astype(jnp.bfloat16) for h in range(heads)], axis=1
+    )
+    dy = jnp.concatenate(
+        [dot(pick, dy_ref[h], ((1,), (0,))).astype(jnp.bfloat16) for h in range(heads)], axis=1
+    )
+    w_both = jnp.concatenate([wg_ref[0], wu_ref[0]], axis=1)
+    pre = dot(x, w_both, ((1,), (0,)))
+    gate_pre = pre[:, :hidden]
+    up_pre = pre[:, hidden:]
+    back_proj = dot(dy, wd_ref[0], ((1,), (1,)))
+    sigmoid_gate = jax.nn.sigmoid(gate_pre)
+    silu_gate = gate_pre * sigmoid_gate
+    active = silu_gate * up_pre
+    route_part = jnp.sum(active * back_proj, axis=1, keepdims=True)
+    route_row = jnp.sum(jnp.where(chosen, route_part, 0.0), axis=0, keepdims=True)
+    droute_ref[...] += jnp.where(routes_ref[...] == expert, route_row, 0.0)
+    d_active = scale_w * back_proj
+    d_gate = d_active * up_pre * sigmoid_gate * (1.0 + gate_pre * (1.0 - sigmoid_gate))
+    d_up = d_active * silu_gate
+    d_both = jnp.concatenate([d_gate, d_up], axis=1).astype(jnp.bfloat16)
+    weighted = (scale_w * active).astype(jnp.bfloat16)
+    back_ref[pl.ds(start, rows), :] = dot(d_both, w_both, ((1,), (1,))).astype(jnp.bfloat16)
+    grad_both = dot(x, d_both, ((0,), (0,))).astype(jnp.bfloat16)
+    gg_ref[0] = grad_both[:, :hidden]
+    gu_ref[0] = grad_both[:, hidden:]
+    gd_ref[0] = dot(weighted, dy, ((0,), (0,))).astype(jnp.bfloat16)
+
+    @pl.when(expert == experts - 1)
+    def _():
+        for h in range(heads):
+            dmoe_ref[h] = dot(
+                pick_ref[...], back_ref[:, h * quarter : (h + 1) * quarter], ((0,), (0,))
+            ).astype(jnp.bfloat16)
+
+
+def run_experts(routes_t, weight_t, x, dy, w_gate, w_up, w_down):
+    local, width, hidden = w_gate.shape
+    heads, total, quarter = x.shape
+    shard_count = lax.axis_size("seq")
+    rows = -(-shard_count * CAP // 16) * 16
+    whole = lambda *shape: pl.BlockSpec(shape, lambda e: (0,) * len(shape))
+    wide = pl.BlockSpec((1, width, hidden), lambda e: (e, 0, 0))
+    tall = pl.BlockSpec((1, hidden, width), lambda e: (e, 0, 0))
+    return pl.pallas_call(
+        expert_kernel,
+        grid=(local,),
+        in_specs=[
+            whole(*routes_t.shape),
+            whole(*weight_t.shape),
+            whole(*x.shape),
+            whole(*dy.shape),
+            wide,
+            wide,
+            tall,
+        ],
+        out_specs=[wide, wide, tall, whole(*x.shape), whole(*weight_t.shape)],
+        out_shape=[
+            jax.ShapeDtypeStruct(w_gate.shape, jnp.bfloat16),
+            jax.ShapeDtypeStruct(w_up.shape, jnp.bfloat16),
+            jax.ShapeDtypeStruct(w_down.shape, jnp.bfloat16),
+            jax.ShapeDtypeStruct(x.shape, jnp.bfloat16),
+            jax.ShapeDtypeStruct(weight_t.shape, jnp.float32),
+        ],
+        scratch_shapes=[
+            pltpu.VMEM((local, total), jnp.float32),
+            pltpu.VMEM((local, total), jnp.float32),
+            pltpu.VMEM((local * rows, total), jnp.bfloat16),
+            pltpu.VMEM((local * rows, width), jnp.bfloat16),
+        ],
+        compiler_params=pltpu.CompilerParams(vmem_limit_bytes=60 << 20),
+        name="experts",
+    )(routes_t, weight_t, x, dy, w_gate, w_up, w_down)
+
+
+def gathered_experts(moe_in, grad_out, routes, route_weight, w_gate, w_up, w_down):
+    local = w_gate.shape[0]
+    both = jnp.stack([moe_in, grad_out])
+    by_seq = lax.all_gather(both, "seq", axis=1, tiled=True)
+    x, dy = jnp.moveaxis(lax.all_gather(by_seq, "head", axis=0), 0, 1)
+    tables = jnp.concatenate(
+        [routes.astype(jnp.float32).T, route_weight.astype(jnp.float32).T], axis=0
+    )
+    tables = lax.all_gather(tables, "seq", axis=1, tiled=True)
+    top = routes.shape[1]
+    routes_t = tables[:top].astype(jnp.int32) - lax.axis_index("seq") * local
+    grad_gate, grad_up, grad_down, d_moe, d_route = run_experts(
+        routes_t, tables[top:], x, dy, w_gate, w_up, w_down
+    )
+    by_head = lax.psum_scatter(d_moe, "head", scatter_dimension=0, tiled=True)
+    d_moe_in = lax.psum_scatter(by_head, "seq", scatter_dimension=1, tiled=True)[0]
+    d_route = lax.psum(d_route, "head")
+    d_route = lax.psum_scatter(d_route, "seq", scatter_dimension=1, tiled=True)
+    d_route_weight = d_route.T.astype(jnp.bfloat16)
+    return (d_moe_in, d_route_weight, grad_gate, grad_up, grad_down)
+
+
+def shards(moe_in, grad_out, routes, route_weight, w_gate, w_up, w_down, queries, key_value):
+    gathered_rows = lax.axis_size("seq") * moe_in.shape[0]
+    experts = gathered_experts if gathered_rows <= EXPERTS * CAP else dispatched_experts
+    d_moe_in, d_route_weight, grad_gate, grad_up, grad_down = experts(
+        moe_in, grad_out, routes, route_weight, w_gate, w_up, w_down
+    )
+    d_queries, d_key_value = attention(grad_out, d_moe_in, queries, key_value)
     return (d_moe_in, d_route_weight, grad_gate, grad_up, grad_down, d_queries, d_key_value)
 
 

time: 398 us -> 240 us (0.60)
  matrix products: 90.7 us -> 3.33 us
  blocking collectives: 108 us -> 23.7 us
  Pallas kernels: 0 us -> 40.8 us
  other arithmetic: 27.5 us -> 6.52 us
  waiting for transfers between devices: 115 us -> 131 us
  local copies, waits for them, and re-layouts: 19.5 us -> 7.42 us
  starting transfers between devices: 22.5 us -> 13.1 us
    all_to_all x3 -> x0, blocking collectives: 90.7 us -> none  [the longest x1 43.2 us: shards(): lax.all_to_all(place_rows(by_token, moe_in), 'seq', split_axis=0, concat_...]
    dot_general x13 -> x0, matrix products: 82.4 us -> none  [the longest x1 15.1 us: shards(): jnp.einsum('secf,edf->secd', d_up, w_up, preferred_element_type=jnp.float32)]
    pallas_call x0 -> x1, Pallas kernels: none -> 40.8 us  [run_experts(): pl.pallas_call(expert_kernel, grid=(local,), in_specs=[whole(*routes_t.sh...]
    unnamed x3 -> x6, waiting for transfers between devices: 0.05 us -> 35.4 us
    all_to_all x2 -> x0, waiting for transfers between devices: 19 us -> none  [the longest x1 19 us: shards(): lax.all_to_all(rows_quarter, 'seq', split_axis=0, concat_axis=0, tiled=True)]
    another operation x4 -> x2, other arithmetic: 18.2 us -> 1.71 us  [the longest x1 1.7 us: gathered_experts(): both = jnp.stack([moe_in, grad_out])]
    all_gather x0 -> x1, blocking collectives: none -> 13.1 us  [gathered_experts(): tables = lax.all_gather(tables, 'seq', axis=1, tiled=True)]
    reduce_scatter x1 -> x2, waiting for transfers between devices: 15.2 us -> 23.4 us  [the longest x1 12.7 us: gathered_experts(): lax.psum_scatter(by_head, 'seq', scatter_dimension=1, tiled=True)[0]]
  transfers between devices with their start and end apart: 13 -> 11, of which waited for: 7 -> 7; matrix products, arithmetic and copies ran while one was open for 13% -> 4% of each run, Pallas kernels for 0% -> 0%
where the time goes in v1:
time: 240 us
  waiting for transfers between devices  131 us (55%)
  Pallas kernels  40.8 us (17%)
  blocking collectives  23.7 us (10%)
  between operations  14 us (6%)
  starting transfers between devices  13.1 us (5%)
  local copies, waits for them, and re-layouts  7.42 us (3%)
  other arithmetic  6.52 us (3%)
  matrix products  3.33 us (1%)
    pallas_call x1, Pallas kernels, run_experts(): pl.pallas_call(expert_kernel, grid=(local,), in_specs=[whole(*routes_t.sh...  40.8 us
    all_gather x1, waiting for transfers between devices, gathered_experts(): x, dy = jnp.moveaxis(lax.all_gather(by_seq, 'head', axis=0), 0, 1)  38 us
    unnamed x6, waiting for transfers between devices  35.4 us
    all_gather x1, waiting for transfers between devices, gathered_experts(): by_seq = lax.all_gather(both, 'seq', axis=1, tiled=True)  31.9 us
    all_gather x1, blocking collectives, gathered_experts(): tables = lax.all_gather(tables, 'seq', axis=1, tiled=True)  13.1 us
    ppermute x6, starting transfers between devices, shifted(): return lax.ppermute(block, axis, route)  12.9 us
    reduce_scatter x1, waiting for transfers between devices, gathered_experts(): lax.psum_scatter(by_head, 'seq', scatter_dimension=1, tiled=True)[0]  12.7 us
    reduce_scatter x1, waiting for transfers between devices, gathered_experts(): d_route = lax.psum_scatter(d_route, 'seq', scatter_dimension=1, tiled=True)  10.7 us
  transfers between devices with their start and end apart: 11, of which 7 were waited for; matrix products, arithmetic and copies ran while one was open for 4% of the time, Pallas kernels for 0%

profile of v1, /device:TPU:0, one launch (start us, length us, event | category | flops | bytes accessed | tf_op | source)
XLA Modules:
  0.0 239.6 jit_solution(7639563239424231689)
XLA Ops:
  7.2 1.7 pad_maximum_fusion
  9.0 31.9 %all-gather.4.cloned.1.call-done = bf16[2,512,512]{2,1,0:T(8,128)(2,1)} async-done(((bf16[2,128,512]{2,1,0:T(8,128)(2,1)}), bf16[2,512,512]{2,1,0:T(8,128)(2,1)}) %all-gather.4.cloned.1.call-update) | async-done | bytes 1048592 | tf_op jit(solution)/shard_map/all_gather | solution.py:343
  40.9 0.7 convert_bitcast_fusion
  41.6 0.7 convert_bitcast_fusion.1
  42.3 13.1 %all_gather.12 = f32[16,512]{1,0:T(8,128)S(1)} all-gather(f32[16,128]{1,0:T(8,128)S(1)} %pad_maximum_fusion.2), channel_id=1, replica_groups=mesh['seq'=4,'head'=4,'rep'=2] {'seq'}, dimensions={1}, use_global_device_ids=true | all-gather | bytes 40960 | tf_op jit(solution)/shard_map/all_gather | solution.py:348
  56.7 38.0 %all-gather.6.cloned.1.call-done = bf16[8,512,512]{2,1,0:T(8,128)(2,1)} async-done(((bf16[2,512,512]{2,1,0:T(8,128)(2,1)}), bf16[8,512,512]{2,1,0:T(8,128)(2,1)}) %all-gather.6.cloned.1.call-update) | async-done | bytes 4194320 | tf_op jit(solution)/shard_map/all_gather | solution.py:344
  94.7 2.6 %copy.28 = bf16[4,2,512,512]{3,2,0,1:T(8,128)(2,1)S(1)} copy(bf16[4,2,512,512]{3,2,1,0:T(8,128)(2,1)} %bitcast.39) | data formatting | bytes 8388608 | tf_op jit(solution)/shard_map/all_gather | solution.py:344
  97.3 2.5 %slice_bitcast_fusion = (bf16[4,512,512]{2,1,0:T(8,128)(2,1)}, bf16[4,512,512]{2,1,0:T(8,128)(2,1)}) fusion(bf16[2,4,512,512]{3,2,1,0:T(8,128)(2,1)S(1)} %bitcast.38), kind=kLoop, calls=%fused_computation.37 | loop fusion | bytes 8388608 | tf_op jit(solution)/shard_map/unstack | solution.py:344
  99.8 40.8 %experts.1 = (bf16[16,2048,128]{2,1,0:T(8,128)(2,1)}, bf16[16,2048,128]{2,1,0:T(8,128)(2,1)}, bf16[16,128,2048]{2,1,0:T(8,128)(2,1)}, bf16[4,512,512]{2,1,0:T(8,128)(2,1)}, f32[8,512]{1,0:T(8,128)}) custom-call(s32[8,512]{1,0:T(8,128)} %fusion.27.routes_ref, f32[8,512]{1,0:T(8,128)} %slice.36.weight_ref, bf16[4,512,512]{2,1,0:T(8,128)(2,1)} %get-tuple-element.302.x_ref, ...), custom_call_target="tpu_custom_call" | custom-call | tf_op jit(solution)/shard_map/experts/pallas_call | solution.py:309
  140.7 35.3 %reduce-scatter.10.cloned.1.call-done = bf16[1,512,512]{2,1,0:T(8,128)(2,1)} async-done(((bf16[4,512,512]{2,1,0:T(8,128)(2,1)}), bf16[1,512,512]{2,1,0:T(8,128)(2,1)}) %reduce-scatter.10.cloned.1.call-update) | async-done | bytes 524304
  176.1 3.4 %collective-permute-start.2 = (bf16[128,128]{1,0:T(8,128)(2,1)S(1)}, bf16[128,128]{1,0:T(8,128)(2,1)S(1)}, u32[]{:S(2)}, u32[]{:S(2)}) collective-permute-start(bf16[128,128]{1,0:T(8,128)(2,1)S(1)} %bitcast.43), channel_id=1, source_target_pairs={{0,8},{8,16},{16,24},{1,9},{9,17},{17,25},{2,10},{10,18},{18,26},{... | collective-permute-start | bytes 98312 | tf_op jit(solution)/shard_map/ppermute | solution.py:16
  179.5 4.3 %collective-permute-start.1 = (bf16[128,128]{1,0:T(8,128)(2,1)S(1)}, bf16[128,128]{1,0:T(8,128)(2,1)S(1)}, u32[]{:S(2)}, u32[]{:S(2)}) collective-permute-start(bf16[128,128]{1,0:T(8,128)(2,1)S(1)} %bitcast.44), channel_id=1, source_target_pairs={{0,16},{8,24},{1,17},{9,25},{2,18},{10,26},{3,19},{11,27},{4,20},{... | collective-permute-start | bytes 98312 | tf_op jit(solution)/shard_map/ppermute | solution.py:16
  183.8 1.3 collective-permute-start
  186.0 1.3 collective-permute-done
  187.5 12.7 %reduce-scatter.6.cloned.1.call-done = bf16[1,128,512]{2,1,0:T(8,128)(2,1)} async-done(((bf16[1,512,512]{2,1,0:T(8,128)(2,1)}), bf16[1,128,512]{2,1,0:T(8,128)(2,1)}) %reduce-scatter.6.cloned.1.call-update) | async-done | bytes 131088 | tf_op jit(solution)/shard_map/reduce_scatter | solution.py:355
  200.2 0.9 add_convert_fusion
  201.4 4.7 %while.18 = (s32[]{:T(128)}, f32[512,128]{0,1:T(8,128)S(1)}, bf16[1024,64]{0,1:T(8,128)(2,1)S(1)}, s32[]{:T(128)}, bf16[1024,64]{1,0:T(8,128)(2,1)S(1)}, /*index...) while((s32[]{:T(128)}, f32[512,128]{0,1:T(8,128)S(1)}, ...), condition=%wide.region_8.9_spmd.clone, body=%wide.region_4.8_spmd.clone.sunk | while | flops 173786624 | bytes 10980585 | solution.py:204
  206.2 1.3 collective-permute-start.5
  207.5 1.3 collective-permute-start.4
  208.8 1.3 collective-permute-start.3
  210.1 10.7 %reduce-scatter.8.cloned.1.call-done = f32[8,128]{1,0:T(8,128)} async-done(((f32[8,512]{1,0:T(8,128)}), f32[8,128]{1,0:T(8,128)}) %reduce-scatter.8.cloned.1.call-update) | async-done | bytes 4112 | tf_op jit(solution)/shard_map/reduce_scatter | solution.py:357
  220.9 10.5 %psum.8 = bf16[8,128]{1,0:T(8,128)(2,1)} all-reduce(f32[8,128]{1,0:T(8,128)} %reduce-scatter.8.cloned.1.call-done), channel_id=1, replica_groups=mesh['seq'=4,'head'=4,'rep'=2] {'head'}, use_global_device_ids=true, to_apply=%region_2.0 | all-reduce | flops 1024 | bytes 6144 | tf_op jit(solution)/shard_map/psum | solution.py:356
  231.5 0.9 reshape.67
  232.4 0.6 fusion.26
  (56 shorter events, 7.5 us)
Async XLA Ops:
  7.2 33.7 %all-gather.4.cloned.1.call-start = ((), (), s32[]{:S(2)}) async-start(), calls=%async_computation.3 | async-start | bytes 1310720 | tf_op jit(solution)/shard_map/all_gather | solution.py:343
  8.9 85.7 %all-gather.6.cloned.1.call-start = ((), (), s32[]{:S(2)}) async-start(), calls=%async_computation.5 | async-start | bytes 5242880 | tf_op jit(solution)/shard_map/all_gather | solution.py:344
  40.9 135.2 %reduce-scatter.10.cloned.1.call-start = ((), (), s32[]{:S(2)}) async-start(), calls=%async_computation.7 | async-start | bytes 2621440
  99.8 76.3 %copy-start.2 = (bf16[128,1,128]{2,0,1:T(8,128)(2,1)S(1)}, bf16[128,1,128]{2,0,1:T(8,128)(2,1)}, u32[]{:S(2)}) copy-start(bf16[128,1,128]{2,0,1:T(8,128)(2,1)} %param.19) | copy-start | bytes 98308
  99.8 85.3 %copy-start.1 = (bf16[128,512]{1,0:T(8,128)(2,1)S(1)}, bf16[128,512]{1,0:T(8,128)(2,1)}, u32[]{:S(2)}) copy-start(bf16[128,512]{1,0:T(8,128)(2,1)} %param.18) | copy-start | bytes 393220
  99.8 100.4 %copy-start = (bf16[128,512]{1,0:T(8,128)(2,1)S(1)}, bf16[128,512]{1,0:T(8,128)(2,1)}, u32[]{:S(2)}) copy-start(bf16[128,512]{1,0:T(8,128)(2,1)} %param.12) | copy-start | bytes 393220
  140.7 59.5 %reduce-scatter.6.cloned.1.call-start = ((), (), s32[]{:S(2)}) async-start(), calls=%async_computation.4 | async-start | bytes 655360 | tf_op jit(solution)/shard_map/reduce_scatter | solution.py:355
  176.1 44.8 %reduce-scatter.8.cloned.1.call-start = ((), (), s32[]{:S(2)}) async-start(), calls=%async_computation.6 | async-start | bytes 20480 | tf_op jit(solution)/shard_map/reduce_scatter | solution.py:357
  176.1 9.2 %collective-permute-start.2 = (bf16[128,128]{1,0:T(8,128)(2,1)S(1)}, bf16[128,128]{1,0:T(8,128)(2,1)S(1)}, u32[]{:S(2)}, u32[]{:S(2)}) collective-permute-start(bf16[128,128]{1,0:T(8,128)(2,1)S(1)} %bitcast.43), channel_id=1, source_target_pairs={{0,8},{8,16},{16,24},{1,9},{9,17},{17,25},{2,10},{10,18},{18,26},{... | collective-permute-start | bytes 98312 | tf_op jit(solution)/shard_map/ppermute | solution.py:16
  179.5 6.5 %collective-permute-start.1 = (bf16[128,128]{1,0:T(8,128)(2,1)S(1)}, bf16[128,128]{1,0:T(8,128)(2,1)S(1)}, u32[]{:S(2)}, u32[]{:S(2)}) collective-permute-start(bf16[128,128]{1,0:T(8,128)(2,1)S(1)} %bitcast.44), channel_id=1, source_target_pairs={{0,16},{8,24},{1,17},{9,25},{2,18},{10,26},{3,19},{11,27},{4,20},{... | collective-permute-start | bytes 98312 | tf_op jit(solution)/shard_map/ppermute | solution.py:16
  183.8 3.5 %collective-permute-start = (bf16[128,128]{1,0:T(8,128)(2,1)S(1)}, bf16[128,128]{1,0:T(8,128)(2,1)S(1)}, u32[]{:S(2)}, u32[]{:S(2)}) collective-permute-start(bf16[128,128]{1,0:T(8,128)(2,1)S(1)} %bitcast.45), channel_id=1, source_target_pairs={{0,24},{1,25},{2,26},{3,27},{4,28},{5,29},{6,30},{7,31}} | collective-permute-start | bytes 98312 | tf_op jit(solution)/shard_map/ppermute | solution.py:16
  206.2 26.2 %collective-permute-start.5 = (bf16[128,128]{1,0:T(8,128)(2,1)S(1)}, bf16[128,128]{1,0:T(8,128)(2,1)S(1)}, u32[]{:S(2)}, u32[]{:S(2)}) collective-permute-start(bf16[128,128]{1,0:T(8,128)(2,1)S(1)} %get-tuple-element.304), channel_id=1, source_target_pairs={{24,0},{25,1},{26,2},{27,3},{28,4},{29,5},{30,6},{31,7}} | collective-permute-start | bytes 98312 | tf_op jit(solution)/shard_map/ppermute | solution.py:16
  207.5 24.9 %collective-permute-start.4 = (bf16[128,128]{1,0:T(8,128)(2,1)S(1)}, bf16[128,128]{1,0:T(8,128)(2,1)S(1)}, u32[]{:S(2)}, u32[]{:S(2)}) collective-permute-start(bf16[128,128]{1,0:T(8,128)(2,1)S(1)} %get-tuple-element.305), channel_id=1, source_target_pairs={{16,0},{24,8},{17,1},{25,9},{18,2},{26,10},{19,3},{27,11},{20,4},{... | collective-permute-start | bytes 98312 | tf_op jit(solution)/shard_map/ppermute | solution.py:16
  208.8 23.6 %collective-permute-start.3 = (bf16[128,128]{1,0:T(8,128)(2,1)S(1)}, bf16[128,128]{1,0:T(8,128)(2,1)S(1)}, u32[]{:S(2)}, u32[]{:S(2)}) collective-permute-start(bf16[128,128]{1,0:T(8,128)(2,1)S(1)} %get-tuple-element.303), channel_id=1, source_target_pairs={{8,0},{16,8},{24,16},{9,1},{17,9},{25,17},{10,2},{18,10},{26,18},{... | collective-permute-start | bytes 98312 | tf_op jit(solution)/shard_map/ppermute | solution.py:16
Sparse Core Ops, SparseCore 0:
  10.1 30.6 all-gather.3
  42.7 51.9 all-gather.5
  140.8 35.1 reduce-scatter.9
  178.7 21.4 reduce-scatter.5
  202.9 17.9 reduce-scatter.7

commit v2 on v1

--- a/solution.py
+++ b/solution.py
@@ -8,6 +8,7 @@
 EXPERTS = 64
 WIN = 512
 CAP = 18
+MESH = pl.DeviceIdType.MESH
 
 
 def shifted(block, axis, distance):
@@ -138,23 +139,20 @@
     return (d_moe_in, d_route_weight, grad_gate, grad_up, grad_down)
 
 
-def attention(grad_out, d_moe_in, queries, key_value):
+def attend(grad_out, d_moe_in, queries, window, first_shard):
     tokens = grad_out.shape[0]
-    head_dim = key_value.shape[2] // 2
+    head_dim = window.shape[1] // 2
     per_group = queries.shape[1] // head_dim
-    reach = min(WIN // tokens, lax.axis_size("seq") - 1)
     scale = head_dim ** (-0.5)
     d_hidden = (grad_out.astype(jnp.float32) + d_moe_in.astype(jnp.float32)).astype(jnp.bfloat16)
     query_rows = queries.reshape(tokens * per_group, head_dim)
     grad_rows = d_hidden.reshape(tokens * per_group, head_dim)
-    own_rows = key_value.reshape(tokens, 2 * head_dim)
-    window = fetch_window(own_rows, reach)
     key_rows = window[:, :head_dim]
     value_rows = window[:, head_dim:]
     contract_last = (((1,), (1,)), ((), ()))
     contract_first = (((0,), (0,)), ((), ()))
     seq_index = lax.axis_index("seq")
-    key_pos = (seq_index - reach) * tokens + jnp.arange((reach + 1) * tokens, dtype=jnp.int32)
+    key_pos = first_shard * tokens + jnp.arange(window.shape[0], dtype=jnp.int32)
     row_total = tokens * per_group
     block_rows = min(512, row_total)
     block_count = row_total // block_rows
@@ -199,12 +197,21 @@
         d_query_all = lax.dynamic_update_slice_in_dim(d_query_all, d_query_blk, begin, 0)
         return (d_window, d_query_all)
 
-    window_start = jnp.zeros(((reach + 1) * tokens, 2 * head_dim), jnp.float32)
+    window_start = jnp.zeros(window.shape, jnp.float32)
     query_start = jnp.zeros((row_total, head_dim), jnp.bfloat16)
     d_window, d_query_all = lax.fori_loop(0, block_count, attend_block, (window_start, query_start))
     d_queries = d_query_all.reshape(tokens, per_group * head_dim)
+    return (d_queries, d_window)
+
+
+def attention(grad_out, d_moe_in, queries, key_value):
+    tokens = grad_out.shape[0]
+    reach = min(WIN // tokens, lax.axis_size("seq") - 1)
+    window = fetch_window(key_value.reshape(tokens, key_value.shape[2]), reach)
+    first_shard = lax.axis_index("seq") - reach
+    d_queries, d_window = attend(grad_out, d_moe_in, queries, window, first_shard)
     d_own = return_window(d_window, reach, tokens)
-    d_key_value = d_own.astype(jnp.bfloat16).reshape(tokens, 1, 2 * head_dim)
+    d_key_value = d_own.astype(jnp.bfloat16).reshape(key_value.shape)
     return (d_queries, d_key_value)
 
 
@@ -213,10 +220,8 @@
 
 
 def expert_kernel(
-    routes_ref,
-    weight_ref,
-    x_ref,
-    dy_ref,
+    tables_ref,
+    tokens_ref,
     wg_ref,
     wu_ref,
     wd_ref,
@@ -224,6 +229,8 @@
     gu_ref,
     gd_ref,
     dmoe_ref,
+    routes_ref,
+    weight_ref,
     droute_ref,
     rank_ref,
     dense_ref,
@@ -232,13 +239,20 @@
 ):
     expert = pl.program_id(0)
     experts = pl.num_programs(0)
-    heads, total, quarter = x_ref.shape
+    _, heads, total, quarter = tokens_ref.shape
+    shard_count, double_top, shard = tables_ref.shape
+    top = double_top // 2
     hidden = wg_ref.shape[2]
     rows = pick_ref.shape[0] // rank_ref.shape[0]
     local = rank_ref.shape[0]
 
     @pl.when(expert == 0)
     def _():
+        first = (lax.axis_index("seq") * local).astype(jnp.float32)
+        for s in range(shard_count):
+            columns = slice(s * shard, (s + 1) * shard)
+            routes_ref[:, columns] = tables_ref[s, :top, :] - first
+            weight_ref[:, columns] = tables_ref[s, top:, :]
         for index in range(local):
             hit = routes_ref[...] == index
             named = jnp.sum(hit.astype(jnp.float32), axis=0, keepdims=True)
@@ -263,10 +277,10 @@
         jnp.where(chosen, dense_ref[pl.ds(expert, 1), :], 0.0), axis=1, keepdims=True
     )
     x = jnp.concatenate(
-        [dot(pick, x_ref[h], ((1,), (0,))).astype(jnp.bfloat16) for h in range(heads)], axis=1
+        [dot(pick, tokens_ref[0, h], ((1,), (0,))).astype(jnp.bfloat16) for h in range(heads)], axis=1
     )
     dy = jnp.concatenate(
-        [dot(pick, dy_ref[h], ((1,), (0,))).astype(jnp.bfloat16) for h in range(heads)], axis=1
+        [dot(pick, tokens_ref[1, h], ((1,), (0,))).astype(jnp.bfloat16) for h in range(heads)], axis=1
     )
     w_both = jnp.concatenate([wg_ref[0], wu_ref[0]], axis=1)
     pre = dot(x, w_both, ((1,), (0,)))
@@ -278,7 +292,7 @@
     active = silu_gate * up_pre
     route_part = jnp.sum(active * back_proj, axis=1, keepdims=True)
     route_row = jnp.sum(jnp.where(chosen, route_part, 0.0), axis=0, keepdims=True)
-    droute_ref[...] += jnp.where(routes_ref[...] == expert, route_row, 0.0)
+    droute_ref[...] += jnp.where(routes_ref[...] == expert.astype(jnp.float32), route_row, 0.0)
     d_active = scale_w * back_proj
     d_gate = d_active * up_pre * sigmoid_gate * (1.0 + gate_pre * (1.0 - sigmoid_gate))
     d_up = d_active * silu_gate
@@ -293,40 +307,43 @@
     @pl.when(expert == experts - 1)
     def _():
         for h in range(heads):
-            dmoe_ref[h] = dot(
-                pick_ref[...], back_ref[:, h * quarter : (h + 1) * quarter], ((0,), (0,))
-            ).astype(jnp.bfloat16)
-
-
-def run_experts(routes_t, weight_t, x, dy, w_gate, w_up, w_down):
+            columns = slice(h * quarter, (h + 1) * quarter)
+            summed = dot(pick_ref[...], back_ref[:, columns], ((0,), (0,))).astype(jnp.bfloat16)
+            for s in range(shard_count):
+                dmoe_ref[h, s, :shard, :] = summed[s * shard : (s + 1) * shard]
+                share = droute_ref[:, s * shard : (s + 1) * shard]
+                share = jnp.concatenate([share, jnp.zeros((16 - top, shard), jnp.float32)], axis=0)
+                if quarter > shard:
+                    blank = jnp.zeros((16, quarter - shard), jnp.float32)
+                    share = jnp.concatenate([share, blank], axis=1)
+                dmoe_ref[h, s, shard:, :] = share.astype(jnp.bfloat16)
+
+
+def run_experts(tables, tokens, w_gate, w_up, w_down):
     local, width, hidden = w_gate.shape
-    heads, total, quarter = x.shape
-    shard_count = lax.axis_size("seq")
+    _, heads, total, quarter = tokens.shape
+    shard_count, double_top, shard = tables.shape
+    top = double_top // 2
     rows = -(-shard_count * CAP // 16) * 16
     whole = lambda *shape: pl.BlockSpec(shape, lambda e: (0,) * len(shape))
     wide = pl.BlockSpec((1, width, hidden), lambda e: (e, 0, 0))
     tall = pl.BlockSpec((1, hidden, width), lambda e: (e, 0, 0))
+    back_shape = (heads, shard_count, shard + 16, quarter)
     return pl.pallas_call(
         expert_kernel,
         grid=(local,),
-        in_specs=[
-            whole(*routes_t.shape),
-            whole(*weight_t.shape),
-            whole(*x.shape),
-            whole(*dy.shape),
-            wide,
-            wide,
-            tall,
-        ],
-        out_specs=[wide, wide, tall, whole(*x.shape), whole(*weight_t.shape)],
+        in_specs=[whole(*tables.shape), whole(*tokens.shape), wide, wide, tall],
+        out_specs=[wide, wide, tall, whole(*back_shape)],
         out_shape=[
             jax.ShapeDtypeStruct(w_gate.shape, jnp.bfloat16),
             jax.ShapeDtypeStruct(w_up.shape, jnp.bfloat16),
             jax.ShapeDtypeStruct(w_down.shape, jnp.bfloat16),
-            jax.ShapeDtypeStruct(x.shape, jnp.bfloat16),
-            jax.ShapeDtypeStruct(weight_t.shape, jnp.float32),
+            jax.ShapeDtypeStruct(back_shape, jnp.bfloat16),
         ],
         scratch_shapes=[
+            pltpu.VMEM((top, total), jnp.float32),
+            pltpu.VMEM((top, total), jnp.float32),
+            pltpu.VMEM((top, total), jnp.float32),
             pltpu.VMEM((local, total), jnp.float32),
             pltpu.VMEM((local, total), jnp.float32),
             pltpu.VMEM((local * rows, total), jnp.bfloat16),
@@ -334,35 +351,397 @@
         ],
         compiler_params=pltpu.CompilerParams(vmem_limit_bytes=60 << 20),
         name="experts",
-    )(routes_t, weight_t, x, dy, w_gate, w_up, w_down)
-
-
-def gathered_experts(moe_in, grad_out, routes, route_weight, w_gate, w_up, w_down):
-    local = w_gate.shape[0]
-    both = jnp.stack([moe_in, grad_out])
-    by_seq = lax.all_gather(both, "seq", axis=1, tiled=True)
-    x, dy = jnp.moveaxis(lax.all_gather(by_seq, "head", axis=0), 0, 1)
-    tables = jnp.concatenate(
+    )(tables, tokens, w_gate, w_up, w_down)
+
+
+def head_neighbours():
+    head = lax.axis_index("head")
+    return head, head + 1 - 2 * (head % 2), (head + 2) % 4, (head + 3 - 2 * (head % 2)) % 4
+
+
+def inside(index, count):
+    return (index >= 0) & (index < count)
+
+
+def greet(along, across):
+    seq = lax.axis_index("seq")
+    count = lax.axis_size("seq")
+    barrier = pltpu.get_barrier_semaphore()
+    for peer in across:
+        pl.semaphore_signal(barrier, inc=1, device_id={"head": peer}, device_id_type=MESH)
+    for step in along:
+
+        @pl.when(inside(seq + step, count))
+        def _():
+            pl.semaphore_signal(
+                barrier, inc=1, device_id={"seq": seq + step}, device_id_type=MESH
+            )
+
+    ends = (seq == 0).astype(jnp.int32) + (seq == count - 1).astype(jnp.int32)
+    pl.semaphore_wait(barrier, len(across) + len(along) - ends)
+
+
+def send(source, target, send_sem, recv_sem, peer):
+    return pltpu.make_async_remote_copy(
+        src_ref=source,
+        dst_ref=target,
+        send_sem=send_sem,
+        recv_sem=recv_sem,
+        device_id=peer,
+        device_id_type=MESH,
+    )
+
+
+def gather_kernel(
+    in_ref,
+    grad_ref,
+    table_ref,
+    kv_ref,
+    tokens_ref,
+    tables_ref,
+    window_ref,
+    own_sem,
+    line_send,
+    line_recv,
+    square_send,
+    square_recv,
+):
+    seq = lax.axis_index("seq")
+    count = lax.axis_size("seq")
+    shard = in_ref.shape[0]
+    half = shard // 2
+    head, beside, above, corner = head_neighbours()
+
+    def piece(of, p):
+        return tokens_ref.at[:, of, pl.ds(p * shard, shard), :]
+
+    def upper(of, p):
+        return tokens_ref.at[:, of, pl.ds(p * shard, half), :]
+
+    def lower(of, p):
+        return tokens_ref.at[:, of, pl.ds(p * shard + half, half), :]
+
+    own_rows = pl.ds(seq * shard, shard)
+    own = [
+        pltpu.make_async_copy(in_ref, tokens_ref.at[0, head, own_rows, :], own_sem.at[0]),
+        pltpu.make_async_copy(grad_ref, tokens_ref.at[1, head, own_rows, :], own_sem.at[1]),
+        pltpu.make_async_copy(table_ref, tables_ref.at[seq], own_sem.at[2]),
+        pltpu.make_async_copy(kv_ref, window_ref.at[seq], own_sem.at[3]),
+    ]
+    for copy in own:
+        copy.start()
+    greet((-1, 1), (beside, above))
+    for copy in own:
+        copy.wait()
+
+    def line(way, p, to):
+        refs = (piece(head, p), tables_ref.at[p], window_ref.at[p])
+        return [
+            send(ref, ref, line_send.at[way, j, p], line_recv.at[way, j, p], {"seq": to})
+            for j, ref in enumerate(refs)
+        ]
+
+    def square(kind, ref, p, to):
+        return send(ref, ref, square_send.at[kind, p], square_recv.at[kind, p], {"head": to})
+
+    def forward(p):
+        square(0, piece(beside, p), p, beside).wait_recv()
+        square(2, upper(beside, p), p, above).start()
+        square(1, piece(above, p), p, above).wait_recv()
+        square(3, lower(above, p), p, beside).start()
+
+    ways = ((0, 1), (1, -1))
+    for k in range(count):
+        for way, step in ways:
+            p = seq - step * k
+
+            @pl.when(inside(p, count))
+            def _():
+                if k > 0:
+                    for copy in line(way, p, seq - step):
+                        copy.wait_recv()
+
+                @pl.when(inside(seq + step, count))
+                def _():
+                    for copy in line(way, p, seq + step):
+                        copy.start()
+
+                if k > 0 or way == 0:
+                    square(0, piece(head, p), p, beside).start()
+                    square(1, piece(head, p), p, above).start()
+
+        if k > 0:
+            for way, step in ways:
+                if k > 1 or way == 0:
+                    p = seq - step * (k - 1)
+                    pl.when(inside(p, count))(lambda p=p: forward(p))
+    for way, step in ways:
+        if count > 1 or way == 0:
+            p = seq - step * (count - 1)
+            pl.when(inside(p, count))(lambda p=p: forward(p))
+    for p in range(count):
+        square(2, upper(corner, p), p, above).wait_recv()
+        square(3, lower(corner, p), p, beside).wait_recv()
+        square(0, piece(head, p), p, beside).wait_send()
+        square(1, piece(head, p), p, above).wait_send()
+        square(2, upper(beside, p), p, above).wait_send()
+        square(3, lower(above, p), p, beside).wait_send()
+    for k in range(count):
+        for way, step in ways:
+            p = seq - step * k
+
+            @pl.when(inside(p, count) & inside(seq + step, count))
+            def _():
+                for copy in line(way, p, seq + step):
+                    copy.wait_send()
+
+
+def gather_tokens(moe_in, grad_out, table, key_value):
+    heads = lax.axis_size("head")
+    count = lax.axis_size("seq")
+    shard, quarter = moe_in.shape
+    return pl.pallas_call(
+        gather_kernel,
+        in_specs=[pl.BlockSpec(memory_space=pltpu.VMEM)] * 4,
+        out_specs=[pl.BlockSpec(memory_space=pltpu.VMEM)] * 3,
+        out_shape=[
+            jax.ShapeDtypeStruct((2, heads, count * shard, quarter), jnp.bfloat16),
+            jax.ShapeDtypeStruct((count,) + table.shape, jnp.float32),
+            jax.ShapeDtypeStruct((count,) + key_value.shape, jnp.bfloat16),
+        ],
+        scratch_shapes=[
+            pltpu.SemaphoreType.DMA((4,)),
+            pltpu.SemaphoreType.DMA((2, 3, count)),
+            pltpu.SemaphoreType.DMA((2, 3, count)),
+            pltpu.SemaphoreType.DMA((4, count)),
+            pltpu.SemaphoreType.DMA((4, count)),
+        ],
+        compiler_params=pltpu.CompilerParams(collective_id=0, has_side_effects=True),
+        name="gather_tokens",
+    )(moe_in, grad_out, table, key_value)
+
+
+def reduce_kernel(
+    part_ref,
+    total_ref,
+    beside_half,
+    above_half,
+    beside_full,
+    above_full,
+    to_beside,
+    to_above,
+    to_line,
+    from_line,
+    send_sem,
+    recv_sem,
+):
+    seq = lax.axis_index("seq")
+    count = lax.axis_size("seq")
+    half = beside_half.shape[1]
+    head, beside, above, corner = head_neighbours()
+    greet((-1, 1), (beside, above))
+
+    def pair(kind, source, target, p, peer):
+        return send(source, target, send_sem.at[kind, p], recv_sem.at[kind, p], peer)
+
+    def first(p):
+        return (
+            pair(
+                0,
+                part_ref.at[corner, p, pl.ds(0, half), :],
+                beside_half.at[p],
+                p,
+                {"head": beside},
+            ),
+            pair(
+                1,
+                part_ref.at[corner, p, pl.ds(half, part_ref.shape[2] - half), :],
+                above_half.at[p],
+                p,
+                {"head": above},
+            ),
+        )
+
+    def second(p):
+        return (
+            pair(2, to_beside.at[p], beside_full.at[p], p, {"head": beside}),
+            pair(3, to_above.at[p], above_full.at[p], p, {"head": above}),
+        )
+
+    def line(way, p, to):
+        return pair(4 + way, to_line.at[p], from_line.at[way, p], p, {"seq": to})
+
+    def each(body):
+        for k in reversed(range(count)):
+            for way, step in ((0, 1), (1, -1)):
+                if k > 0 or way == 0:
+                    p = seq + step * k
+                    pl.when(inside(p, count))(lambda k=k, way=way, step=step, p=p: body(k, way, step, p))
+
+    def start_first(k, way, step, p):
+        for copy in first(p):
+            copy.start()
+
+    def add_first(k, way, step, p):
+        from_beside, from_above = first(p)
+        via_beside, via_above = second(p)
+        from_beside.wait_recv()
+        to_above[p, :half, :] = (
+            part_ref[above, p, :half, :].astype(jnp.float32)
+            + beside_half[p].astype(jnp.float32)
+        ).astype(jnp.bfloat16)
+        to_above[p, half:, :] = part_ref[above, p, half:, :]
+        via_above.start()
+        from_above.wait_recv()
+        to_beside[p, :half, :] = part_ref[beside, p, :half, :]
+        to_beside[p, half:, :] = (
+            part_ref[beside, p, half:, :].astype(jnp.float32) + above_half[p].astype(jnp.float32)
+        ).astype(jnp.bfloat16)
+        via_beside.start()
+
+    def add_second(k, way, step, p):
+        for copy in second(p):
+            copy.wait_recv()
+        summed = (
+            part_ref[head, p].astype(jnp.float32)
+            + beside_full[p].astype(jnp.float32)
+            + above_full[p].astype(jnp.float32)
+        )
+        if k > 0:
+            to_line[p] = summed.astype(jnp.bfloat16)
+
+            @pl.when(inside(seq - step, count))
+            def _():
+                line(way, p, seq - step).wait_recv()
+                to_line[p] = (summed + from_line[way, p].astype(jnp.float32)).astype(jnp.bfloat16)
+
+            line(way, p, seq + step).start()
+        else:
+            for other in range(count):
+
+                @pl.when(seq == other)
+                def _():
+                    result = summed
+                    if other > 0:
+                        line(0, p, seq - 1).wait_recv()
+                        result = result + from_line[0, p].astype(jnp.float32)
+                    if other < count - 1:
+                        line(1, p, seq + 1).wait_recv()
+                        result = result + from_line[1, p].astype(jnp.float32)
+                    total_ref[...] = result.astype(jnp.bfloat16)
+
+    def finish(k, way, step, p):
+        for copy in first(p) + second(p):
+            copy.wait_send()
+        if k > 0:
+            line(way, p, seq + step).wait_send()
+
+    each(start_first)
+    each(add_first)
+    each(add_second)
+    each(finish)
+
+
+def reduce_tokens(part):
+    _, count, rows, quarter = part.shape
+    half = (rows - 16) // 2
+    block = lambda *lead: pltpu.VMEM(lead + (rows, quarter), jnp.bfloat16)
+    return pl.pallas_call(
+        reduce_kernel,
+        in_specs=[pl.BlockSpec(memory_space=pltpu.VMEM)],
+        out_specs=pl.BlockSpec(memory_space=pltpu.VMEM),
+        out_shape=jax.ShapeDtypeStruct((rows, quarter), jnp.bfloat16),
+        scratch_shapes=[
+            pltpu.VMEM((count, half, quarter), jnp.bfloat16),
+            pltpu.VMEM((count, rows - half, quarter), jnp.bfloat16),
+            block(count),
+            block(count),
+            block(count),
+            block(count),
+            block(count),
+            block(2, count),
+            pltpu.SemaphoreType.DMA((6, count)),
+            pltpu.SemaphoreType.DMA((6, count)),
+        ],
+        compiler_params=pltpu.CompilerParams(collective_id=1, has_side_effects=True),
+        name="reduce_tokens",
+    )(part)
+
+
+def return_kernel(part_ref, total_ref, landed, send_sem, recv_sem):
+    seq = lax.axis_index("seq")
+    count = lax.axis_size("seq")
+    barrier = pltpu.get_barrier_semaphore()
+    for offset in range(1, count):
+        pl.semaphore_signal(
+            barrier, inc=1, device_id={"seq": (seq + offset) % count}, device_id_type=MESH
+        )
+    pl.semaphore_wait(barrier, count - 1)
+    copies = []
+    for offset in range(1, count):
+        to = (seq + offset) % count
+        copies.append(
+            send(
+                part_ref.at[to],
+                landed.at[offset],
+                send_sem.at[offset],
+                recv_sem.at[offset],
+                {"seq": to},
+            )
+        )
+        copies[-1].start()
+    summed = part_ref[seq].astype(jnp.float32)
+    for offset, copy in enumerate(copies, 1):
+        copy.wait_recv()
+        summed = summed + landed[offset].astype(jnp.float32)
+    total_ref[...] = summed.astype(jnp.bfloat16)
+    for copy in copies:
+        copy.wait_send()
+
+
+def return_shards(part):
+    count, shard, width = part.shape
+    return pl.pallas_call(
+        return_kernel,
+        in_specs=[pl.BlockSpec(memory_space=pltpu.VMEM)],
+        out_specs=pl.BlockSpec(memory_space=pltpu.VMEM),
+        out_shape=jax.ShapeDtypeStruct((shard, width), jnp.bfloat16),
+        scratch_shapes=[
+            pltpu.VMEM(part.shape, jnp.bfloat16),
+            pltpu.SemaphoreType.DMA((count,)),
+            pltpu.SemaphoreType.DMA((count,)),
+        ],
+        compiler_params=pltpu.CompilerParams(collective_id=2, has_side_effects=True),
+        name="return_shards",
+    )(part)
+
+
+def gathered_layer(moe_in, grad_out, routes, route_weight, w_gate, w_up, w_down, queries, key_value):
+    shard, top = routes.shape
+    table = jnp.concatenate(
         [routes.astype(jnp.float32).T, route_weight.astype(jnp.float32).T], axis=0
     )
-    tables = lax.all_gather(tables, "seq", axis=1, tiled=True)
-    top = routes.shape[1]
-    routes_t = tables[:top].astype(jnp.int32) - lax.axis_index("seq") * local
-    grad_gate, grad_up, grad_down, d_moe, d_route = run_experts(
-        routes_t, tables[top:], x, dy, w_gate, w_up, w_down
-    )
-    by_head = lax.psum_scatter(d_moe, "head", scatter_dimension=0, tiled=True)
-    d_moe_in = lax.psum_scatter(by_head, "seq", scatter_dimension=1, tiled=True)[0]
-    d_route = lax.psum(d_route, "head")
-    d_route = lax.psum_scatter(d_route, "seq", scatter_dimension=1, tiled=True)
-    d_route_weight = d_route.T.astype(jnp.bfloat16)
-    return (d_moe_in, d_route_weight, grad_gate, grad_up, grad_down)
+    own_rows = key_value.reshape(shard, key_value.shape[2])
+    tokens, tables, window = gather_tokens(moe_in, grad_out, table, own_rows)
+    grad_gate, grad_up, grad_down, d_moe = run_experts(tables, tokens, w_gate, w_up, w_down)
+    summed = reduce_tokens(d_moe)
+    d_moe_in = summed[:shard]
+    d_route_weight = summed[shard : shard + top, :shard].T
+    d_queries, d_window = attend(
+        grad_out, d_moe_in, queries, window.reshape(-1, window.shape[2]), 0
+    )
+    d_own = return_shards(d_window.astype(jnp.bfloat16).reshape(window.shape))
+    d_key_value = d_own.reshape(key_value.shape)
+    return (d_moe_in, d_route_weight, grad_gate, grad_up, grad_down, d_queries, d_key_value)
 
 
 def shards(moe_in, grad_out, routes, route_weight, w_gate, w_up, w_down, queries, key_value):
     gathered_rows = lax.axis_size("seq") * moe_in.shape[0]
-    experts = gathered_experts if gathered_rows <= EXPERTS * CAP else dispatched_experts
-    d_moe_in, d_route_weight, grad_gate, grad_up, grad_down = experts(
+    if gathered_rows <= EXPERTS * CAP and lax.axis_size("head") == 4:
+        return gathered_layer(
+            moe_in, grad_out, routes, route_weight, w_gate, w_up, w_down, queries, key_value
+        )
+    d_moe_in, d_route_weight, grad_gate, grad_up, grad_down = dispatched_experts(
         moe_in, grad_out, routes, route_weight, w_gate, w_up, w_down
     )
     d_queries, d_key_value = attention(grad_out, d_moe_in, queries, key_value)

time: 240 us -> 139 us (0.58)
  waiting for transfers between devices: 131 us -> 0 us
  Pallas kernels: 40.8 us -> 124 us
  blocking collectives: 23.7 us -> 0 us
  between operations: 14 us -> 0.76 us
  starting transfers between devices: 13.1 us -> 0 us
  local copies, waits for them, and re-layouts: 7.42 us -> 4.91 us
    pallas_call x1 -> x4, Pallas kernels: 40.8 us -> 124 us  [the longest x1 45.3 us: gather_tokens(): pl.pallas_call(gather_kernel, in_specs=[pl.BlockSpec(memory_space=pltpu.V...]
    all_gather x2 -> x0, waiting for transfers between devices: 69.9 us -> none  [the longest x1 38 us: gathered_experts(): x, dy = jnp.moveaxis(lax.all_gather(by_seq, 'head', axis=0), 0, 1)]
    unnamed x6 -> x0, waiting for transfers between devices: 35.4 us -> none
    reduce_scatter x2 -> x0, waiting for transfers between devices: 23.4 us -> none  [the longest x1 12.7 us: gathered_experts(): lax.psum_scatter(by_head, 'seq', scatter_dimension=1, tiled=True)[0]]
    all_gather x1 -> x0, blocking collectives: 13.1 us -> none  [gathered_experts(): tables = lax.all_gather(tables, 'seq', axis=1, tiled=True)]
    ppermute x6 -> x0, starting transfers between devices: 12.9 us -> none  [shifted(): return lax.ppermute(block, axis, route)]
    psum x1 -> x0, blocking collectives: 10.5 us -> none  [gathered_experts(): d_route = lax.psum(d_route, 'head')]
    all_gather x1 -> x0, local copies, waits for them, and re-layouts: 2.64 us -> none  [gathered_experts(): x, dy = jnp.moveaxis(lax.all_gather(by_seq, 'head', axis=0), 0, 1)]
  transfers between devices with their start and end apart: 11 -> 0, of which waited for: 7 -> 0; matrix products, arithmetic and copies ran while one was open for 4% -> 0% of each run, Pallas kernels for 0% -> 0%
where the time goes in v2:
time: 139 us; the launch traced here: 138 us
  Pallas kernels  124 us (89%)
  local copies, waits for them, and re-layouts  4.91 us (4%)
  other arithmetic  4.75 us (3%)
  matrix products  3.27 us (2%)
    pallas_call x1, Pallas kernels, gather_tokens(): pl.pallas_call(gather_kernel, in_specs=[pl.BlockSpec(memory_space=pltpu.V...  45.3 us
    pallas_call x1, Pallas kernels, run_experts(): pl.pallas_call(expert_kernel, grid=(local,), in_specs=[whole(*tables.shap...  40.7 us
    pallas_call x1, Pallas kernels, reduce_tokens(): pl.pallas_call(reduce_kernel, in_specs=[pl.BlockSpec(memory_space=pltpu.V...  31.1 us
    pallas_call x1, Pallas kernels, return_shards(): pl.pallas_call(return_kernel, in_specs=[pl.BlockSpec(memory_space=pltpu.V...  7.32 us

profile of v2, /device:TPU:0, one launch (start us, length us, event | category | flops | bytes accessed | tf_op | source)
XLA Modules:
  0.0 138.2 jit_solution(14209283493948270691)
XLA Ops:
  0.6 0.7 convert_bitcast_fusion
  1.3 0.7 convert_bitcast_fusion.1
  2.0 0.6 pad_maximum_fusion.table_ref
  2.6 45.3 %gather_tokens.1 = (bf16[2,4,512,512]{3,2,1,0:T(8,128)(2,1)}, f32[4,16,128]{2,1,0:T(8,128)}, bf16[4,128,128]{2,1,0:T(8,128)(2,1)}) custom-call(bf16[128,512]{1,0:T(8,128)(2,1)} %in_ref.1, bf16[128,512]{1,0:T(8,128)(2,1)} %grad_ref.1, f32[16,128]{1,0:T(8,128)} %pad_maximum_fusion.table_ref, bf16[128,128]{1,0:T(8,128)(2,1)} %bitcast.28), custom_call_target="tpu_custom_call" | custom-call | tf_op jit(solution)/shard_map/gather_tokens/pallas_call | solution.py:503
  47.9 40.7 %experts.1 = (bf16[16,2048,128]{2,1,0:T(8,128)(2,1)}, bf16[16,2048,128]{2,1,0:T(8,128)(2,1)}, bf16[16,128,2048]{2,1,0:T(8,128)(2,1)}, bf16[4,4,144,512]{3,2,1,0:T(8,128)(2,1)}) custom-call(f32[4,16,128]{2,1,0:T(8,128)} %get-tuple-element.245.tables_ref, bf16[2,4,512,512]{3,2,1,0:T(8,128)(2,1)} %get-tuple-element.246.tokens_ref, ...), custom_call_target="tpu_custom_call" | custom-call | tf_op jit(solution)/shard_map/experts/pallas_call | solution.py:332
  88.6 31.1 %reduce_tokens.1 = bf16[144,512]{1,0:T(8,128)(2,1)} custom-call(bf16[4,4,144,512]{3,2,1,0:T(8,128)(2,1)} %get-tuple-element.247.part_ref), custom_call_target="tpu_custom_call" | custom-call | tf_op jit(solution)/shard_map/reduce_tokens/pallas_call | solution.py:649
  119.8 1.6 %add_convert_fusion = (bf16[128,512]{1,0:T(8,128)(2,1)S(1)}, bf16[128,512]{1,0:T(8,128)(2,1)}) fusion(bf16[128,512]{1,0:T(8,128)(2,1)S(1)} %copy-done, bf16[144,512]{1,0:T(8,128)(2,1)} %reduce_tokens.1), kind=kLoop, calls=%fused_computation.37 | loop fusion | flops 262144 | bytes 524288 | tf_op jit(solution)/shard_map/convert_element_type | solution.py:147
  121.9 4.6 %while.19 = (s32[]{:T(128)}, f32[512,128]{0,1:T(8,128)S(1)}, bf16[1024,64]{0,1:T(8,128)(2,1)S(1)}, s32[]{:T(128)}, bf16[1024,64]{1,0:T(8,128)(2,1)S(1)}, /*index...) while((s32[]{:T(128)}, f32[512,128]{0,1:T(8,128)S(1)}, ...), condition=%wide.region_4.5_spmd.clone.clone, body=%wide.region_0.4_spmd.clone.clone.sunk | while | flops 173514240 | bytes 10975433 | solution.py:202
  121.9 0.4 fusion.54
  122.6 0.3 multiply_reduce_fusion.2
  122.9 0.3 multiply_convert_fusion.2
  123.2 0.3 fusion.57
  123.5 0.3 fusion.56
  123.9 0.2 fusion.58
  124.2 0.4 fusion.54
  124.9 0.3 multiply_reduce_fusion.2
  125.2 0.3 multiply_convert_fusion.2
  125.5 0.3 fusion.57
  125.8 0.3 fusion.56
  126.7 0.9 reshape.74
  127.5 0.7 copy.19
  128.3 7.3 %return_shards.1 = bf16[128,128]{1,0:T(8,128)(2,1)} custom-call(bf16[4,128,128]{2,1,0:T(8,128)(2,1)} %bitcast.25), custom_call_target="tpu_custom_call" | custom-call | tf_op jit(solution)/shard_map/return_shards/pallas_call | solution.py:704
  135.6 1.2 slice_bitcast_fusion
  136.9 1.4 copy.31
  (20 shorter events, 1.5 us)
Async XLA Ops:
  47.9 71.9 %copy-start = (bf16[128,512]{1,0:T(8,128)(2,1)S(1)}, bf16[128,512]{1,0:T(8,128)(2,1)}, u32[]{:S(2)}) copy-start(bf16[128,512]{1,0:T(8,128)(2,1)} %grad_ref.1) | copy-start | bytes 393220
  47.9 73.6 %copy-start.1 = (bf16[4,128,128]{2,1,0:T(8,128)(2,1)S(1)}, bf16[4,128,128]{2,1,0:T(8,128)(2,1)}, u32[]{:S(2)}) copy-start(bf16[4,128,128]{2,1,0:T(8,128)(2,1)} %get-tuple-element.251) | copy-start | bytes 393220
  47.9 73.7 %copy-start.2 = (bf16[128,512]{1,0:T(8,128)(2,1)S(1)}, bf16[128,512]{1,0:T(8,128)(2,1)}, u32[]{:S(2)}) copy-start(bf16[128,512]{1,0:T(8,128)(2,1)} %param.18) | copy-start | bytes 393220

commit v3 on v2

--- a/solution.py
+++ b/solution.py
@@ -237,8 +237,8 @@
     pick_ref,
     back_ref,
 ):
-    expert = pl.program_id(0)
-    experts = pl.num_programs(0)
+    group = pl.program_id(0)
+    per_step = wg_ref.shape[0]
     _, heads, total, quarter = tokens_ref.shape
     shard_count, double_top, shard = tables_ref.shape
     top = double_top // 2
@@ -246,7 +246,7 @@
     rows = pick_ref.shape[0] // rank_ref.shape[0]
     local = rank_ref.shape[0]
 
-    @pl.when(expert == 0)
+    @pl.when(group == 0)
     def _():
         first = (lax.axis_index("seq") * local).astype(jnp.float32)
         for s in range(shard_count):
@@ -269,42 +269,66 @@
         droute_ref[...] = jnp.zeros_like(droute_ref)
 
     slots = lax.broadcasted_iota(jnp.int32, (rows, total), 0).astype(jnp.float32)
-    chosen = rank_ref[pl.ds(expert, 1), :] == slots
-    pick = chosen.astype(jnp.float32).astype(jnp.bfloat16)
-    start = pl.multiple_of(expert * rows, rows)
-    pick_ref[pl.ds(start, rows), :] = pick
-    scale_w = jnp.sum(
-        jnp.where(chosen, dense_ref[pl.ds(expert, 1), :], 0.0), axis=1, keepdims=True
-    )
-    x = jnp.concatenate(
-        [dot(pick, tokens_ref[0, h], ((1,), (0,))).astype(jnp.bfloat16) for h in range(heads)], axis=1
-    )
-    dy = jnp.concatenate(
-        [dot(pick, tokens_ref[1, h], ((1,), (0,))).astype(jnp.bfloat16) for h in range(heads)], axis=1
-    )
-    w_both = jnp.concatenate([wg_ref[0], wu_ref[0]], axis=1)
-    pre = dot(x, w_both, ((1,), (0,)))
-    gate_pre = pre[:, :hidden]
-    up_pre = pre[:, hidden:]
-    back_proj = dot(dy, wd_ref[0], ((1,), (1,)))
-    sigmoid_gate = jax.nn.sigmoid(gate_pre)
-    silu_gate = gate_pre * sigmoid_gate
-    active = silu_gate * up_pre
-    route_part = jnp.sum(active * back_proj, axis=1, keepdims=True)
-    route_row = jnp.sum(jnp.where(chosen, route_part, 0.0), axis=0, keepdims=True)
-    droute_ref[...] += jnp.where(routes_ref[...] == expert.astype(jnp.float32), route_row, 0.0)
-    d_active = scale_w * back_proj
-    d_gate = d_active * up_pre * sigmoid_gate * (1.0 + gate_pre * (1.0 - sigmoid_gate))
-    d_up = d_active * silu_gate
-    d_both = jnp.concatenate([d_gate, d_up], axis=1).astype(jnp.bfloat16)
-    weighted = (scale_w * active).astype(jnp.bfloat16)
-    back_ref[pl.ds(start, rows), :] = dot(d_both, w_both, ((1,), (1,))).astype(jnp.bfloat16)
-    grad_both = dot(x, d_both, ((0,), (0,))).astype(jnp.bfloat16)
-    gg_ref[0] = grad_both[:, :hidden]
-    gu_ref[0] = grad_both[:, hidden:]
-    gd_ref[0] = dot(weighted, dy, ((0,), (0,))).astype(jnp.bfloat16)
-
-    @pl.when(expert == experts - 1)
+
+    def choose(j):
+        expert = group * per_step + j
+        chosen = rank_ref[pl.ds(expert, 1), :] == slots
+        pick = chosen.astype(jnp.float32).astype(jnp.bfloat16)
+        scale_w = jnp.sum(
+            jnp.where(chosen, dense_ref[pl.ds(expert, 1), :], 0.0), axis=1, keepdims=True
+        )
+        return expert, chosen, pick, scale_w
+
+    choices = [choose(j) for j in range(per_step)]
+    picks = jnp.concatenate([pick for _, _, pick, _ in choices], axis=0)
+    x_all, dy_all = (
+        jnp.concatenate(
+            [
+                dot(picks, tokens_ref[part, h], ((1,), (0,))).astype(jnp.bfloat16)
+                for h in range(heads)
+            ],
+            axis=1,
+        )
+        for part in range(2)
+    )
+    start = pl.multiple_of(group * (per_step * rows), rows)
+    pick_ref[pl.ds(start, per_step * rows), :] = picks
+    forward = []
+    for j, (expert, chosen, _, scale_w) in enumerate(choices):
+        x = x_all[j * rows : (j + 1) * rows]
+        dy = dy_all[j * rows : (j + 1) * rows]
+        w_both = jnp.concatenate([wg_ref[j], wu_ref[j]], axis=1)
+        pre = dot(x, w_both, ((1,), (0,)))
+        back_proj = dot(dy, wd_ref[j], ((1,), (1,)))
+        forward.append((x, dy, w_both, pre, back_proj))
+    backward = []
+    for (expert, chosen, _, scale_w), (x, dy, w_both, pre, back_proj) in zip(choices, forward):
+        gate_pre = pre[:, :hidden]
+        up_pre = pre[:, hidden:]
+        sigmoid_gate = jax.nn.sigmoid(gate_pre)
+        silu_gate = gate_pre * sigmoid_gate
+        active = silu_gate * up_pre
+        route_part = jnp.sum(active * back_proj, axis=1, keepdims=True)
+        route_row = jnp.sum(jnp.where(chosen, route_part, 0.0), axis=0, keepdims=True)
+        droute_ref[...] += jnp.where(
+            routes_ref[...] == expert.astype(jnp.float32), route_row, 0.0
+        )
+        d_active = scale_w * back_proj
+        d_gate = d_active * up_pre * sigmoid_gate * (1.0 + gate_pre * (1.0 - sigmoid_gate))
+        d_up = d_active * silu_gate
+        d_both = jnp.concatenate([d_gate, d_up], axis=1).astype(jnp.bfloat16)
+        backward.append((d_both, (scale_w * active).astype(jnp.bfloat16)))
+    for j, (x, dy, w_both, _, _) in enumerate(forward):
+        d_both, weighted = backward[j]
+        back_ref[pl.ds(start + j * rows, rows), :] = dot(d_both, w_both, ((1,), (1,))).astype(
+            jnp.bfloat16
+        )
+        grad_both = dot(x, d_both, ((0,), (0,))).astype(jnp.bfloat16)
+        gg_ref[j] = grad_both[:, :hidden]
+        gu_ref[j] = grad_both[:, hidden:]
+        gd_ref[j] = dot(weighted, dy, ((0,), (0,))).astype(jnp.bfloat16)
+
+    @pl.when(group == pl.num_programs(0) - 1)
     def _():
         for h in range(heads):
             columns = slice(h * quarter, (h + 1) * quarter)
@@ -326,12 +350,13 @@
     top = double_top // 2
     rows = -(-shard_count * CAP // 16) * 16
     whole = lambda *shape: pl.BlockSpec(shape, lambda e: (0,) * len(shape))
-    wide = pl.BlockSpec((1, width, hidden), lambda e: (e, 0, 0))
-    tall = pl.BlockSpec((1, hidden, width), lambda e: (e, 0, 0))
+    per_step = 2 if local % 2 == 0 else 1
+    wide = pl.BlockSpec((per_step, width, hidden), lambda e: (e, 0, 0))
+    tall = pl.BlockSpec((per_step, hidden, width), lambda e: (e, 0, 0))
     back_shape = (heads, shard_count, shard + 16, quarter)
     return pl.pallas_call(
         expert_kernel,
-        grid=(local,),
+        grid=(local // per_step,),
         in_specs=[whole(*tables.shape), whole(*tokens.shape), wide, wide, tall],
         out_specs=[wide, wide, tall, whole(*back_shape)],
         out_shape=[
@@ -668,14 +693,57 @@
     )(part)
 
 
-def return_kernel(part_ref, total_ref, landed, send_sem, recv_sem):
+def attend_kernel(
+    grad_ref,
+    summed_ref,
+    query_ref,
+    window_ref,
+    d_query_ref,
+    total_ref,
+    part_ref,
+    landed,
+    send_sem,
+    recv_sem,
+):
     seq = lax.axis_index("seq")
-    count = lax.axis_size("seq")
+    count, shard, width = window_ref.shape
+    head_dim = width // 2
+    per_group = query_ref.shape[1] // head_dim
+    scale = head_dim ** (-0.5)
     barrier = pltpu.get_barrier_semaphore()
     for offset in range(1, count):
         pl.semaphore_signal(
             barrier, inc=1, device_id={"seq": (seq + offset) % count}, device_id_type=MESH
         )
+    window = jnp.concatenate([window_ref[p] for p in range(count)], axis=0)
+    key_rows = window[:, :head_dim]
+    value_rows = window[:, head_dim:]
+    d_hidden = (
+        grad_ref[...].astype(jnp.float32) + summed_ref[:shard, :].astype(jnp.float32)
+    ).astype(jnp.bfloat16)
+    position = seq * shard + lax.broadcasted_iota(jnp.int32, (shard, count * shard), 0)
+    key_pos = lax.broadcasted_iota(jnp.int32, (shard, count * shard), 1)
+    visible = (key_pos <= position) & (key_pos > position - WIN)
+    d_keys = jnp.zeros((head_dim, count * shard), jnp.float32)
+    d_values = jnp.zeros((head_dim, count * shard), jnp.float32)
+    d_query = []
+    for g in range(per_group):
+        columns = slice(g * head_dim, (g + 1) * head_dim)
+        query = query_ref[:, columns]
+        grad = d_hidden[:, columns]
+        scores = dot(query, key_rows, ((1,), (1,))) * scale
+        scores = jnp.where(visible, scores, -1e30)
+        raised = jnp.exp(scores - jnp.max(scores, axis=1, keepdims=True))
+        probs = raised / jnp.sum(raised, axis=1, keepdims=True)
+        d_probs = dot(grad, value_rows, ((1,), (1,)))
+        row_dot = jnp.sum(probs * d_probs, axis=1, keepdims=True)
+        d_scores = (probs * (d_probs - row_dot) * scale).astype(jnp.bfloat16)
+        d_query.append(dot(d_scores, key_rows, ((1,), (0,))).astype(jnp.bfloat16))
+        d_keys = d_keys + dot(query, d_scores, ((0,), (0,)))
+        d_values = d_values + dot(grad, probs.astype(jnp.bfloat16), ((0,), (0,)))
+    d_window = jnp.concatenate([d_keys, d_values], axis=0).T.astype(jnp.bfloat16)
+    for p in range(count):
+        part_ref[p] = d_window[p * shard : (p + 1) * shard]
     pl.semaphore_wait(barrier, count - 1)
     copies = []
     for offset in range(1, count):
@@ -690,6 +758,7 @@
             )
         )
         copies[-1].start()
+    d_query_ref[...] = jnp.concatenate(d_query, axis=1)
     summed = part_ref[seq].astype(jnp.float32)
     for offset, copy in enumerate(copies, 1):
         copy.wait_recv()
@@ -699,21 +768,25 @@
         copy.wait_send()
 
 
-def return_shards(part):
-    count, shard, width = part.shape
+def attend_and_return(grad_out, summed, queries, window):
+    count, shard, width = window.shape
     return pl.pallas_call(
-        return_kernel,
-        in_specs=[pl.BlockSpec(memory_space=pltpu.VMEM)],
-        out_specs=pl.BlockSpec(memory_space=pltpu.VMEM),
-        out_shape=jax.ShapeDtypeStruct((shard, width), jnp.bfloat16),
+        attend_kernel,
+        in_specs=[pl.BlockSpec(memory_space=pltpu.VMEM)] * 4,
+        out_specs=[pl.BlockSpec(memory_space=pltpu.VMEM)] * 2,
+        out_shape=[
+            jax.ShapeDtypeStruct(queries.shape, jnp.bfloat16),
+            jax.ShapeDtypeStruct((shard, width), jnp.bfloat16),
+        ],
         scratch_shapes=[
-            pltpu.VMEM(part.shape, jnp.bfloat16),
+            pltpu.VMEM(window.shape, jnp.bfloat16),
+            pltpu.VMEM(window.shape, jnp.bfloat16),
             pltpu.SemaphoreType.DMA((count,)),
             pltpu.SemaphoreType.DMA((count,)),
         ],
         compiler_params=pltpu.CompilerParams(collective_id=2, has_side_effects=True),
-        name="return_shards",
-    )(part)
+        name="attend_and_return",
+    )(grad_out, summed, queries, window)
 
 
 def gathered_layer(moe_in, grad_out, routes, route_weight, w_gate, w_up, w_down, queries, key_value):
@@ -727,10 +800,7 @@
     summed = reduce_tokens(d_moe)
     d_moe_in = summed[:shard]
     d_route_weight = summed[shard : shard + top, :shard].T
-    d_queries, d_window = attend(
-        grad_out, d_moe_in, queries, window.reshape(-1, window.shape[2]), 0
-    )
-    d_own = return_shards(d_window.astype(jnp.bfloat16).reshape(window.shape))
+    d_queries, d_own = attend_and_return(grad_out, summed, queries, window)
     d_key_value = d_own.reshape(key_value.shape)
     return (d_moe_in, d_route_weight, grad_gate, grad_up, grad_down, d_queries, d_key_value)
 

time: 139 us -> 127 us (0.914)
  Pallas kernels: 124 us -> 118 us
  matrix products: 3.27 us -> 0 us
  other arithmetic: 4.75 us -> 1.97 us
    pallas_call x2, Pallas kernels: 48 us -> 41.9 us  [the longest x1 33.6 us: run_experts(): pl.pallas_call(expert_kernel, grid=(local // per_step,), in_specs=[whole(...]
    dot_general x10 -> x0, matrix products: 3.27 us -> none  [the longest x2 0.89 us: attend_block(): lax.dot_general(query_blk, key_rows, contract_last, preferred_element_typ...]
    convert_element_type x4 -> x0, other arithmetic: 2.18 us -> none  [the longest x1 1.58 us: attend(): (grad_out.astype(jnp.float32) + d_moe_in.astype(jnp.float32)).astype(jnp....]
    unnamed x7 -> x2, local copies, waits for them, and re-layouts: 1.39 us -> 2.94 us
    slice x1, local copies, waits for them, and re-layouts: 0.11 us -> 1.57 us  [gathered_layer(): d_moe_in = summed[:shard]]
where the time goes in v3:
time: 127 us
  Pallas kernels  118 us (93%)
  local copies, waits for them, and re-layouts  5.75 us (5%)
  other arithmetic  1.97 us (2%)
    pallas_call x1, Pallas kernels, gather_tokens(): pl.pallas_call(gather_kernel, in_specs=[pl.BlockSpec(memory_space=pltpu.V...  45.3 us
    pallas_call x1, Pallas kernels, run_experts(): pl.pallas_call(expert_kernel, grid=(local // per_step,), in_specs=[whole(...  33.6 us
    pallas_call x1, Pallas kernels, reduce_tokens(): pl.pallas_call(reduce_kernel, in_specs=[pl.BlockSpec(memory_space=pltpu.V...  31.1 us
    pallas_call x1, Pallas kernels, attend_and_return(): pl.pallas_call(attend_kernel, in_specs=[pl.BlockSpec(memory_space=pltpu.V...  8.28 us
    unnamed x2, local copies, waits for them, and re-layouts  2.94 us

profile of v3, /device:TPU:0, one launch (start us, length us, event | category | flops | bytes accessed | tf_op | source)
XLA Modules:
  0.0 126.7 jit_solution(6433221681997806481)
XLA Ops:
  0.6 0.7 convert_bitcast_fusion.1
  1.3 0.7 convert_bitcast_fusion
  2.0 0.6 pad_maximum_fusion.table_ref
  2.6 45.3 %gather_tokens.1 = (bf16[2,4,512,512]{3,2,1,0:T(8,128)(2,1)}, f32[4,16,128]{2,1,0:T(8,128)}, bf16[4,128,128]{2,1,0:T(8,128)(2,1)}) custom-call(bf16[128,512]{1,0:T(8,128)(2,1)} %in_ref.1, bf16[128,512]{1,0:T(8,128)(2,1)} %grad_ref.3, f32[16,128]{1,0:T(8,128)} %pad_maximum_fusion.table_ref, bf16[128,128]{1,0:T(8,128)(2,1)} %bitcast.8), custom_call_target="tpu_custom_call" | custom-call | tf_op jit(solution)/shard_map/gather_tokens/pallas_call | solution.py:528
  47.9 33.6 %experts.1 = (bf16[16,2048,128]{2,1,0:T(8,128)(2,1)}, bf16[16,2048,128]{2,1,0:T(8,128)(2,1)}, bf16[16,128,2048]{2,1,0:T(8,128)(2,1)}, bf16[4,4,144,512]{3,2,1,0:T(8,128)(2,1)}) custom-call(f32[4,16,128]{2,1,0:T(8,128)} %get-tuple-element.16.tables_ref, bf16[2,4,512,512]{3,2,1,0:T(8,128)(2,1)} %get-tuple-element.17.tokens_ref, bf16[16,2048,128]{2,1,0:T(8,128)(2,1)} %wg_ref.1, ...), custom_call_target="tpu_custom_call" | custom-call | tf_op jit(solution)/shard_map/experts/pallas_call | solution.py:357
  81.5 31.1 %reduce_tokens.1.summed_ref = bf16[144,512]{1,0:T(8,128)(2,1)} custom-call(bf16[4,4,144,512]{3,2,1,0:T(8,128)(2,1)} %get-tuple-element.18.part_ref), custom_call_target="tpu_custom_call" | custom-call | tf_op jit(solution)/shard_map/reduce_tokens/pallas_call | solution.py:674
  112.7 1.2 slice_bitcast_fusion
  113.9 8.3 %attend_and_return.1 = (bf16[128,512]{1,0:T(8,128)(2,1)}, bf16[128,128]{1,0:T(8,128)(2,1)}) custom-call(bf16[128,512]{1,0:T(8,128)(2,1)} %grad_ref.3, bf16[144,512]{1,0:T(8,128)(2,1)} %reduce_tokens.1.summed_ref, bf16[128,512]{1,0:T(8,128)(2,1)} %query_ref.1, bf16[4,128,128]{2,1,0:T(8,128)(2,1)} %get-tuple-element.22.window_ref), custom_call_target="tpu_custom_call" | custom-call | tf_op jit(solution)/shard_map/attend_and_return/pallas_call | solution.py:773
  122.2 1.6 %slice.6 = bf16[128,512]{1,0:T(8,128)(2,1)} slice(bf16[144,512]{1,0:T(8,128)(2,1)} %reduce_tokens.1.summed_ref), slice={[0:128], [0:512]} | slice | bytes 262144 | tf_op jit(solution)/shard_map/slice | solution.py:801
  123.8 1.6 %copy.18 = bf16[128,512]{1,0:T(8,128)(2,1)} copy(bf16[128,512]{1,0:T(8,128)(2,1)} %get-tuple-element.37) | data formatting | bytes 262144
  125.4 1.4 %copy.19 = bf16[128,1,128]{2,0,1:T(8,128)(2,1)} copy(bf16[128,1,128]{2,0,1:T(8,128)(2,1)} %bitcast.9) | data formatting | bytes 65536

commit v4 on v3

--- a/solution.py
+++ b/solution.py
@@ -350,7 +350,7 @@
     top = double_top // 2
     rows = -(-shard_count * CAP // 16) * 16
     whole = lambda *shape: pl.BlockSpec(shape, lambda e: (0,) * len(shape))
-    per_step = 2 if local % 2 == 0 else 1
+    per_step = 4 if local % 4 == 0 else 1
     wide = pl.BlockSpec((per_step, width, hidden), lambda e: (e, 0, 0))
     tall = pl.BlockSpec((per_step, hidden, width), lambda e: (e, 0, 0))
     back_shape = (heads, shard_count, shard + 16, quarter)
@@ -477,6 +477,8 @@
 
     ways = ((0, 1), (1, -1))
     for k in range(count):
+        if k == 1:
+            forward(seq)
         for way, step in ways:
             p = seq - step * k
 
@@ -495,7 +497,7 @@
                     square(0, piece(head, p), p, beside).start()
                     square(1, piece(head, p), p, above).start()
 
-        if k > 0:
+        if k > 1:
             for way, step in ways:
                 if k > 1 or way == 0:
                     p = seq - step * (k - 1)
@@ -596,12 +598,11 @@
     def line(way, p, to):
         return pair(4 + way, to_line.at[p], from_line.at[way, p], p, {"seq": to})
 
-    def each(body):
-        for k in reversed(range(count)):
-            for way, step in ((0, 1), (1, -1)):
-                if k > 0 or way == 0:
-                    p = seq + step * k
-                    pl.when(inside(p, count))(lambda k=k, way=way, step=step, p=p: body(k, way, step, p))
+    def at(k, body):
+        for way, step in ((0, 1), (1, -1)):
+            if k > 0 or way == 0:
+                p = seq + step * k
+                pl.when(inside(p, count))(lambda way=way, step=step, p=p: body(k, way, step, p))
 
     def start_first(k, way, step, p):
         for copy in first(p):
@@ -661,10 +662,13 @@
         if k > 0:
             line(way, p, seq + step).wait_send()
 
-    each(start_first)
-    each(add_first)
-    each(add_second)
-    each(finish)
+    for turn in range(count + 3):
+        for body, behind in ((add_first, 2), (add_second, 3), (start_first, 0)):
+            k = count - 1 - (turn - behind)
+            if 0 <= k < count:
+                at(k, body)
+    for k in range(count):
+        at(k, finish)
 
 
 def reduce_tokens(part):

time: 127 us -> 126 us (level)
    pallas_call x1, Pallas kernels: 31.1 us -> 28.6 us  [reduce_tokens(): pl.pallas_call(reduce_kernel, in_specs=[pl.BlockSpec(memory_space=pltpu.V...]
where the time goes in v4:
time: 126 us
  Pallas kernels  118 us (94%)
  local copies, waits for them, and re-layouts  5.75 us (5%)
  other arithmetic  1.97 us (2%)
    pallas_call x1, Pallas kernels, gather_tokens(): pl.pallas_call(gather_kernel, in_specs=[pl.BlockSpec(memory_space=pltpu.V...  45.1 us
    pallas_call x1, Pallas kernels, run_experts(): pl.pallas_call(expert_kernel, grid=(local // per_step,), in_specs=[whole(...  34.7 us
    pallas_call x1, Pallas kernels, reduce_tokens(): pl.pallas_call(reduce_kernel, in_specs=[pl.BlockSpec(memory_space=pltpu.V...  28.6 us
    pallas_call x1, Pallas kernels, attend_and_return(): pl.pallas_call(attend_kernel, in_specs=[pl.BlockSpec(memory_space=pltpu.V...  9.4 us
    unnamed x2, local copies, waits for them, and re-layouts  2.94 us

profile of v4, /device:TPU:0, one launch (start us, length us, event | category | flops | bytes accessed | tf_op | source)
XLA Modules:
  0.0 126.1 jit_solution(2095888517956920416)
XLA Ops:
  0.6 0.7 convert_bitcast_fusion.1
  1.3 0.7 convert_bitcast_fusion
  2.0 0.6 pad_maximum_fusion.table_ref
  2.6 45.1 %gather_tokens.1 = (bf16[2,4,512,512]{3,2,1,0:T(8,128)(2,1)}, f32[4,16,128]{2,1,0:T(8,128)}, bf16[4,128,128]{2,1,0:T(8,128)(2,1)}) custom-call(bf16[128,512]{1,0:T(8,128)(2,1)} %in_ref.1, bf16[128,512]{1,0:T(8,128)(2,1)} %grad_ref.3, f32[16,128]{1,0:T(8,128)} %pad_maximum_fusion.table_ref, bf16[128,128]{1,0:T(8,128)(2,1)} %bitcast.8), custom_call_target="tpu_custom_call" | custom-call | tf_op jit(solution)/shard_map/gather_tokens/pallas_call | solution.py:530
  47.7 34.7 %experts.1 = (bf16[16,2048,128]{2,1,0:T(8,128)(2,1)}, bf16[16,2048,128]{2,1,0:T(8,128)(2,1)}, bf16[16,128,2048]{2,1,0:T(8,128)(2,1)}, bf16[4,4,144,512]{3,2,1,0:T(8,128)(2,1)}) custom-call(f32[4,16,128]{2,1,0:T(8,128)} %get-tuple-element.16.tables_ref, bf16[2,4,512,512]{3,2,1,0:T(8,128)(2,1)} %get-tuple-element.17.tokens_ref, bf16[16,2048,128]{2,1,0:T(8,128)(2,1)} %wg_ref.1, ...), custom_call_target="tpu_custom_call" | custom-call | tf_op jit(solution)/shard_map/experts/pallas_call | solution.py:357
  82.3 28.6 %reduce_tokens.1.summed_ref = bf16[144,512]{1,0:T(8,128)(2,1)} custom-call(bf16[4,4,144,512]{3,2,1,0:T(8,128)(2,1)} %get-tuple-element.18.part_ref), custom_call_target="tpu_custom_call" | custom-call | tf_op jit(solution)/shard_map/reduce_tokens/pallas_call | solution.py:678
  111.0 1.2 slice_bitcast_fusion
  112.2 9.4 %attend_and_return.1 = (bf16[128,512]{1,0:T(8,128)(2,1)}, bf16[128,128]{1,0:T(8,128)(2,1)}) custom-call(bf16[128,512]{1,0:T(8,128)(2,1)} %grad_ref.3, bf16[144,512]{1,0:T(8,128)(2,1)} %reduce_tokens.1.summed_ref, bf16[128,512]{1,0:T(8,128)(2,1)} %query_ref.1, bf16[4,128,128]{2,1,0:T(8,128)(2,1)} %get-tuple-element.22.window_ref), custom_call_target="tpu_custom_call" | custom-call | tf_op jit(solution)/shard_map/attend_and_return/pallas_call | solution.py:777
  121.6 1.6 %slice.6 = bf16[128,512]{1,0:T(8,128)(2,1)} slice(bf16[144,512]{1,0:T(8,128)(2,1)} %reduce_tokens.1.summed_ref), slice={[0:128], [0:512]} | slice | bytes 262144 | tf_op jit(solution)/shard_map/slice | solution.py:805
  123.2 1.6 %copy.18 = bf16[128,512]{1,0:T(8,128)(2,1)} copy(bf16[128,512]{1,0:T(8,128)(2,1)} %get-tuple-element.37) | data formatting | bytes 262144
  124.7 1.4 %copy.19 = bf16[128,1,128]{2,0,1:T(8,128)(2,1)} copy(bf16[128,1,128]{2,0,1:T(8,128)(2,1)} %bitcast.9) | data formatting | bytes 65536

commit v5 on v4

--- a/solution.py
+++ b/solution.py
@@ -350,7 +350,7 @@
     top = double_top // 2
     rows = -(-shard_count * CAP // 16) * 16
     whole = lambda *shape: pl.BlockSpec(shape, lambda e: (0,) * len(shape))
-    per_step = 4 if local % 4 == 0 else 1
+    per_step = 2 if local % 2 == 0 else 1
     wide = pl.BlockSpec((per_step, width, hidden), lambda e: (e, 0, 0))
     tall = pl.BlockSpec((per_step, hidden, width), lambda e: (e, 0, 0))
     back_shape = (heads, shard_count, shard + 16, quarter)
@@ -420,7 +420,8 @@
 def gather_kernel(
     in_ref,
     grad_ref,
-    table_ref,
+    routes_ref,
+    weight_ref,
     kv_ref,
     tokens_ref,
     tables_ref,
@@ -450,11 +451,13 @@
     own = [
         pltpu.make_async_copy(in_ref, tokens_ref.at[0, head, own_rows, :], own_sem.at[0]),
         pltpu.make_async_copy(grad_ref, tokens_ref.at[1, head, own_rows, :], own_sem.at[1]),
-        pltpu.make_async_copy(table_ref, tables_ref.at[seq], own_sem.at[2]),
-        pltpu.make_async_copy(kv_ref, window_ref.at[seq], own_sem.at[3]),
+        pltpu.make_async_copy(kv_ref, window_ref.at[seq], own_sem.at[2]),
     ]
     for copy in own:
         copy.start()
+    tables_ref[seq] = jnp.concatenate(
+        [routes_ref[...].astype(jnp.float32), weight_ref[...].astype(jnp.float32)], axis=0
+    )
     greet((-1, 1), (beside, above))
     for copy in own:
         copy.wait()
@@ -523,21 +526,21 @@
                     copy.wait_send()
 
 
-def gather_tokens(moe_in, grad_out, table, key_value):
+def gather_tokens(moe_in, grad_out, routes_t, weight_t, key_value):
     heads = lax.axis_size("head")
     count = lax.axis_size("seq")
     shard, quarter = moe_in.shape
     return pl.pallas_call(
         gather_kernel,
-        in_specs=[pl.BlockSpec(memory_space=pltpu.VMEM)] * 4,
+        in_specs=[pl.BlockSpec(memory_space=pltpu.VMEM)] * 5,
         out_specs=[pl.BlockSpec(memory_space=pltpu.VMEM)] * 3,
         out_shape=[
             jax.ShapeDtypeStruct((2, heads, count * shard, quarter), jnp.bfloat16),
-            jax.ShapeDtypeStruct((count,) + table.shape, jnp.float32),
+            jax.ShapeDtypeStruct((count, 2 * routes_t.shape[0], shard), jnp.float32),
             jax.ShapeDtypeStruct((count,) + key_value.shape, jnp.bfloat16),
         ],
         scratch_shapes=[
-            pltpu.SemaphoreType.DMA((4,)),
+            pltpu.SemaphoreType.DMA((3,)),
             pltpu.SemaphoreType.DMA((2, 3, count)),
             pltpu.SemaphoreType.DMA((2, 3, count)),
             pltpu.SemaphoreType.DMA((4, count)),
@@ -545,7 +548,7 @@
         ],
         compiler_params=pltpu.CompilerParams(collective_id=0, has_side_effects=True),
         name="gather_tokens",
-    )(moe_in, grad_out, table, key_value)
+    )(moe_in, grad_out, routes_t, weight_t, key_value)
 
 
 def reduce_kernel(
@@ -795,11 +798,10 @@
 
 def gathered_layer(moe_in, grad_out, routes, route_weight, w_gate, w_up, w_down, queries, key_value):
     shard, top = routes.shape
-    table = jnp.concatenate(
-        [routes.astype(jnp.float32).T, route_weight.astype(jnp.float32).T], axis=0
-    )
     own_rows = key_value.reshape(shard, key_value.shape[2])
-    tokens, tables, window = gather_tokens(moe_in, grad_out, table, own_rows)
+    tokens, tables, window = gather_tokens(
+        moe_in, grad_out, routes.T, route_weight.T, own_rows
+    )
     grad_gate, grad_up, grad_down, d_moe = run_experts(tables, tokens, w_gate, w_up, w_down)
     summed = reduce_tokens(d_moe)
     d_moe_in = summed[:shard]

time: 126 us -> 123 us (0.976)
  other arithmetic: 1.97 us -> 0 us
    transpose x2 -> x0, other arithmetic: 1.37 us -> none  [the longest x1 0.69 us: gathered_layer(): routes.astype(jnp.float32)]
where the time goes in v5:
time: 123 us
  Pallas kernels  117 us (95%)
  local copies, waits for them, and re-layouts  5.75 us (5%)
    pallas_call x1, Pallas kernels, gather_tokens(): pl.pallas_call(gather_kernel, in_specs=[pl.BlockSpec(memory_space=pltpu.V...  45.1 us
    pallas_call x1, Pallas kernels, run_experts(): pl.pallas_call(expert_kernel, grid=(local // per_step,), in_specs=[whole(...  33.7 us
    pallas_call x1, Pallas kernels, reduce_tokens(): pl.pallas_call(reduce_kernel, in_specs=[pl.BlockSpec(memory_space=pltpu.V...  28.5 us
    pallas_call x1, Pallas kernels, attend_and_return(): pl.pallas_call(attend_kernel, in_specs=[pl.BlockSpec(memory_space=pltpu.V...  9.35 us
    unnamed x2, local copies, waits for them, and re-layouts  2.94 us

profile of v5, /device:TPU:0, one launch (start us, length us, event | category | flops | bytes accessed | tf_op | source)
XLA Modules:
  0.0 122.9 jit_solution(11811269218420285834)
XLA Ops:
  0.6 45.1 %gather_tokens.1 = (bf16[2,4,512,512]{3,2,1,0:T(8,128)(2,1)}, f32[4,16,128]{2,1,0:T(8,128)}, bf16[4,128,128]{2,1,0:T(8,128)(2,1)}) custom-call(bf16[128,512]{1,0:T(8,128)(2,1)} %in_ref.1, bf16[128,512]{1,0:T(8,128)(2,1)} %grad_ref.3, s32[8,128]{1,0:T(8,128)} %bitcast.8, bf16[8,128]{1,0:T(8,128)(2,1)} %bitcast.9, bf16[128,128]{1,0:T(8,128)(2,1)} %bitcast.6), custom_call_target="tpu_custom_call" | custom-call | tf_op jit(solution)/shard_map/gather_tokens/pallas_call | solution.py:533
  45.7 33.7 %experts.1 = (bf16[16,2048,128]{2,1,0:T(8,128)(2,1)}, bf16[16,2048,128]{2,1,0:T(8,128)(2,1)}, bf16[16,128,2048]{2,1,0:T(8,128)(2,1)}, bf16[4,4,144,512]{3,2,1,0:T(8,128)(2,1)}) custom-call(f32[4,16,128]{2,1,0:T(8,128)} %get-tuple-element.16.tables_ref, bf16[2,4,512,512]{3,2,1,0:T(8,128)(2,1)} %get-tuple-element.17.tokens_ref, bf16[16,2048,128]{2,1,0:T(8,128)(2,1)} %wg_ref.1, ...), custom_call_target="tpu_custom_call" | custom-call | tf_op jit(solution)/shard_map/experts/pallas_call | solution.py:357
  79.4 28.5 %reduce_tokens.1.summed_ref = bf16[144,512]{1,0:T(8,128)(2,1)} custom-call(bf16[4,4,144,512]{3,2,1,0:T(8,128)(2,1)} %get-tuple-element.18.part_ref), custom_call_target="tpu_custom_call" | custom-call | tf_op jit(solution)/shard_map/reduce_tokens/pallas_call | solution.py:681
  107.8 1.2 %slice_bitcast_fusion = bf16[128,8]{0,1:T(8,128)(2,1)} fusion(bf16[144,512]{1,0:T(8,128)(2,1)} %reduce_tokens.1.summed_ref), kind=kLoop, calls=%fused_computation | loop fusion | bytes 4096 | tf_op jit(solution)/shard_map/transpose | solution.py:808
  109.1 9.4 %attend_and_return.1 = (bf16[128,512]{1,0:T(8,128)(2,1)}, bf16[128,128]{1,0:T(8,128)(2,1)}) custom-call(bf16[128,512]{1,0:T(8,128)(2,1)} %grad_ref.3, bf16[144,512]{1,0:T(8,128)(2,1)} %reduce_tokens.1.summed_ref, bf16[128,512]{1,0:T(8,128)(2,1)} %query_ref.1, bf16[4,128,128]{2,1,0:T(8,128)(2,1)} %get-tuple-element.22.window_ref), custom_call_target="tpu_custom_call" | custom-call | tf_op jit(solution)/shard_map/attend_and_return/pallas_call | solution.py:780
  118.4 1.6 %slice.6 = bf16[128,512]{1,0:T(8,128)(2,1)} slice(bf16[144,512]{1,0:T(8,128)(2,1)} %reduce_tokens.1.summed_ref), slice={[0:128], [0:512]} | slice | bytes 262144 | tf_op jit(solution)/shard_map/slice | solution.py:807
  120.0 1.6 %copy.18 = bf16[128,512]{1,0:T(8,128)(2,1)} copy(bf16[128,512]{1,0:T(8,128)(2,1)} %get-tuple-element.37) | data formatting | bytes 262144
  121.6 1.4 %copy.19 = bf16[128,1,128]{2,0,1:T(8,128)(2,1)} copy(bf16[128,1,128]{2,0,1:T(8,128)(2,1)} %bitcast.7) | data formatting | bytes 65536
